TPU v7x, 128 devices: a whole 4x4x4 slice. The times are simulated.
128 devices in a mesh: bx: 4 (over y), by: 4 (over x), bz: 8 (over z, core).
Axes of the slice: x: 4, y: 4, z: 4, core: 2. Of those that a mesh axis runs over, the one named last changes fastest.
Arguments:
- position: float32 [3, 128, 128, 2048], P(None, 'bx', 'by', 'bz'), may hold values from -2 to 2
- velocity: float32 [3, 128, 128, 2048], P(None, 'bx', 'by', 'bz'), may hold values from -3 to 3
- density: float32 [128, 128, 2048], P('bx', 'by', 'bz'), may hold values from 0.5 to 2
- energy: float32 [128, 128, 2048], P('bx', 'by', 'bz'), may hold values from 0.1 to 10
- pinned: int32 [128, 128, 2048], P('bx', 'by', 'bz'), may hold values 0 or 1
Outputs:
- velocity_new: float32 [3, 128, 128, 2048], P(None, 'bx', 'by', 'bz')
- accel: float32 [3, 128, 128, 2048], P(None, 'bx', 'by', 'bz')
- relaxed: float32 [3, 128, 128, 2048], P(None, 'bx', 'by', 'bz')
- density_new: float32 [128, 128, 2048], P('bx', 'by', 'bz')
- energy_new: float32 [128, 128, 2048], P('bx', 'by', 'bz')
All inputs are finite; a program needn't handle non-finite values. No bound on the sum of `pinned` on one device may be relied on, other than what follows from the above.
Results may differ from a plain program's by a relative error of at most 0.0003.
Values sent between devices are 32-bit elements; how exact they have to be, the bound alone decides.
A program may use at most 128 MiB of HBM per device.

v0:
```python
import jax
import jax.numpy as jnp
from jax import lax
from jax.sharding import PartitionSpec as P

CG_ITERS = 2
SWEEPS = 3


TIME_STEP = 0.6
RELAX_RATE = 0.8
CONSISTENT = 0.2


def from_behind(x, axis, by):
    length = lax.axis_size(axis)
    pairs = [(i, i + by) for i in range(length) if 0 <= i + by < length]
    return lax.ppermute(x, axis, pairs)


def padded(block, sides, width):
    for axis, dim in sides:
        count = lax.axis_size(axis)
        forward = [(i, i + 1) for i in range(count - 1)]
        backward = [(target, source) for source, target in forward]
        low = lax.ppermute(
            lax.slice_in_dim(block, block.shape[dim] - width, None, axis=dim), axis, forward
        )
        high = lax.ppermute(lax.slice_in_dim(block, 0, width, axis=dim), axis, backward)
        block = jnp.concatenate([low, block, high], axis=dim)
    return block


def shift_triple(along_dim, along, first, second):
    offsets = [0, 0, 0]
    offsets[along_dim] = along
    others = [d for d in range(3) if d != along_dim]
    offsets[others[0]] = first
    offsets[others[1]] = second
    return offsets


def select_at(extended, offsets):
    sizes = extended.shape[-3:]
    return extended[
        ...,
        1 + offsets[0] : sizes[0] - 1 + offsets[0],
        1 + offsets[1] : sizes[1] - 1 + offsets[1],
        1 + offsets[2] : sizes[2] - 1 + offsets[2],
    ]


def corner_force(pressure_ext):
    parts = []
    for along_dim in range(3):
        summed = 0.0
        for first in (0, -1):
            for second in (0, -1):
                summed = (
                    summed
                    + select_at(pressure_ext, shift_triple(along_dim, -1, first, second))
                    - select_at(pressure_ext, shift_triple(along_dim, 0, first, second))
                )
        parts.append(0.25 * summed)
    return jnp.stack(parts)


def node_mass(density_ext):
    summed = 0.0
    for first in (0, -1):
        for second in (0, -1):
            for third in (0, -1):
                summed = summed + select_at(density_ext, [first, second, third])
    return 0.125 * summed


def neighbours(extended):
    summed = 0.0
    for along_dim in range(3):
        for along in (-1, 1):
            summed = summed + select_at(extended, shift_triple(along_dim, along, 0, 0))
    return summed


def divergence(vel_ext):
    summed = 0.0
    for along_dim in range(3):
        for first in (0, 1):
            for second in (0, 1):
                summed = (
                    summed
                    + select_at(vel_ext[along_dim], shift_triple(along_dim, 1, first, second))
                    - select_at(vel_ext[along_dim], shift_triple(along_dim, 0, first, second))
                )
    return 0.25 * summed


def face_flux(packed, along_dim, along):
    speed = 0.0
    for first in (0, 1):
        for second in (0, 1):
            speed = speed + select_at(
                packed[along_dim], shift_triple(along_dim, along, first, second)
            )
    speed = 0.25 * speed
    upper = select_at(packed[3:5], shift_triple(along_dim, along, 0, 0))
    lower = select_at(packed[3:5], shift_triple(along_dim, along - 1, 0, 0))
    return speed * jnp.where(speed > 0, upper, lower)


def remap_cells(packed):
    result = select_at(packed[3:5], [0, 0, 0])
    for along_dim in range(3):
        result = result + face_flux(packed, along_dim, 1) - face_flux(packed, along_dim, 0)
    return result


def inner(first, second):
    return jnp.sum(first * second, axis=(1, 2, 3), keepdims=True)


def lower_cells(values):
    got = from_behind(values[..., -1:, :, :], "bx", 1)
    widened = jnp.concatenate([got, values], axis=-3)
    got = from_behind(widened[..., :, -1:, :], "by", 1)
    widened = jnp.concatenate([got, widened], axis=-2)
    got = from_behind(widened[..., :, :, -1:], "bz", 1)
    widened = jnp.concatenate([got, widened], axis=-1)
    return jnp.pad(widened, [(0, 0)] * (values.ndim - 3) + [(0, 1)] * 3)


def upper_nodes(values):
    got = from_behind(values[..., :1, :, :], "bx", -1)
    widened = jnp.concatenate([values, got], axis=-3)
    got = from_behind(widened[..., :, :1, :], "by", -1)
    widened = jnp.concatenate([widened, got], axis=-2)
    got = from_behind(widened[..., :, :, :1], "bz", -1)
    widened = jnp.concatenate([widened, got], axis=-1)
    return jnp.pad(widened, [(0, 0)] * (values.ndim - 3) + [(1, 0)] * 3)


def mass_apply(vector, masses):
    extended = padded(vector, (("bx", 1), ("by", 2), ("bz", 3)), 1)
    return masses * vector + CONSISTENT * (6.0 * vector + neighbours(extended))


def squares(residual):
    return lax.psum(inner(residual, residual), ("bx", "by", "bz"))


def one_sweep(relaxed, free):
    extended = padded(relaxed, (("bx", 1), ("by", 2), ("bz", 3)), 1)
    return relaxed + RELAX_RATE * free * (neighbours(extended) / 6.0 - relaxed)


def on_device(position, velocity, density, energy, pinned):
    cells = lower_cells(jnp.stack([density, energy]))
    force = corner_force(0.4 * cells[0] * cells[1])
    masses = node_mass(cells[0])
    solution = jnp.zeros_like(force)
    residual = force
    direction = force
    norm_now = squares(residual)
    for step_index in range(CG_ITERS):
        image = mass_apply(direction, masses)
        alpha = norm_now / lax.psum(inner(direction, image), ("bx", "by", "bz"))
        solution = solution + alpha * direction
        residual = residual - alpha * image
        norm_next = squares(residual)
        direction = residual + norm_next / norm_now * direction
        norm_now = norm_next
    velocity_new = velocity + TIME_STEP * solution
    vel_ext = upper_nodes(velocity_new)
    spread = divergence(vel_ext)
    pressure = 0.4 * density * energy
    energy_lag = energy - TIME_STEP * pressure * spread / density
    moved = position + TIME_STEP * velocity_new
    free = 1.0 - pinned.astype(jnp.float32)
    relaxed = moved
    for step_index in range(SWEEPS):
        relaxed = one_sweep(relaxed, free)
    packed = padded(
        jnp.concatenate([relaxed - moved, density[None], (density * energy_lag)[None]]),
        (("bx", 1), ("by", 2), ("bz", 3)),
        1,
    )
    remapped = remap_cells(packed)
    return (velocity_new, solution, relaxed, remapped[0], remapped[1])


def solution(mesh):
    in_specs = (
        P(None, "bx", "by", "bz"),
        P(None, "bx", "by", "bz"),
        P("bx", "by", "bz"),
        P("bx", "by", "bz"),
        P("bx", "by", "bz"),
    )
    out_specs = (
        P(None, "bx", "by", "bz"),
        P(None, "bx", "by", "bz"),
        P(None, "bx", "by", "bz"),
        P("bx", "by", "bz"),
        P("bx", "by", "bz"),
    )
    return jax.shard_map(
        on_device, mesh=mesh, in_specs=in_specs, out_specs=out_specs, check_vma=False
    )
```

profile of v0, /device:TPU:1, one launch (start us, length us, event | category | flops | bytes accessed | tf_op | source)
XLA Modules:
  0.0 638.1 jit_solution(13406718772434215634)
XLA Ops:
  1.6 4.0 collective-permute-start
  8.0 3.1 collective-permute-start.1
  14.1 5.8 collective-permute-start.2
  22.3 3.6 select_maximum_fusion.3
  29.0 4.0 collective-permute-start.3
  34.6 3.7 collective-permute-done.4
  38.5 4.0 collective-permute-start.5
  45.3 4.1 collective-permute-done.6
  52.9 3.0 copy.64
  55.9 3.0 copy.66
  61.2 5.9 collective-permute-start.7
  67.1 7.7 %fusion.120 = f32[32,32,256]{2,1,0:T(8,128)} fusion(f32[34,34,258]{2,1,0:T(8,128)} %slice_bitcast_fusion.7), kind=kLoop, calls=%fused_computation.316 | loop fusion | flops 2097152 | bytes 9437184 | tf_op jit(solution)/shard_map/mul | solution.py:74
  74.8 2.9 copy.65
  77.8 2.9 copy.67
  80.7 16.0 %multiply_reduce_fusion.1 = (f32[3]{0:T(128)}, f32[3]{0:T(128)}, f32[3,32,32,256]{3,2,1,0:T(8,128)}) fusion(f32[1,32,32,256]{3,2,1,0:T(8,128)} %copy-done.4, f32[1,32,32,256]{3,2,1,0:T(8,128)S(1)} %multiply_bitcast_fusion.1, f32[1,32,32,256]{3,2,1,0:T(8,128)S(1)} %get-tuple-element.82, f32[3,34,34,1]{3,2,1,0:T(8,128)} %copy.67, ...), kind=kLoop, calls=%fused_computation.195 | loop fusion | flops 36175864 | bytes 7773304 | tf_op jit(solution)/shard_map/reduce_sum | solution.py:119
  96.7 64.6 %all-reduce.2 = (f32[3,1,1,1]{0,3,2,1:T(1,128)S(1)}, f32[3,1,1,1]{0,3,2,1:T(1,128)S(1)}) all-reduce(f32[3,1,1,1]{0,3,2,1:T(1,128)} %bitcast.58, f32[3,1,1,1]{0,3,2,1:T(1,128)} %bitcast.57), channel_id=1, replica_groups=mesh['bx'=4,'by'=4,'bz'=8] {'bx','by','bz'}, use_global_device_ids=true, to_apply=%region_1.2 | all-reduce | flops 6 | bytes 48 | tf_op jit(solution)/shard_map/psum | solution.py:148
  164.2 63.1 %psum.30 = f32[3,1,1,1]{0,3,2,1:T(1,128)S(1)} all-reduce(f32[3,1,1,1]{0,3,2,1:T(1,128)S(1)} %bitcast.60), channel_id=1, replica_groups=mesh['bx'=4,'by'=4,'bz'=8] {'bx','by','bz'}, use_global_device_ids=true, to_apply=%region_5.6 | all-reduce | flops 3 | bytes 24 | tf_op jit(solution)/shard_map/psum | solution.py:148
  227.3 3.1 multiply_add_fusion.3
  234.4 3.7 collective-permute-done.10
  241.7 3.8 collective-permute-done.12
  248.8 3.0 copy.68
  251.8 5.8 collective-permute-start.13
  257.6 3.0 copy.70
  262.7 2.9 copy.69
  266.4 2.9 copy.71
  269.3 15.8 %fusion.67 = f32[3]{0:T(128)} fusion(f32[3,32,32,256]{3,2,1,0:T(8,128)} %copy-done.5, f32[3,34,34,1]{3,2,1,0:T(8,128)} %copy.71, f32[3,34,1,256]{3,2,1,0:T(1,128)S(1)} %collective-permute-done.12, f32[3,34,1,256]{3,2,1,0:T(1,128)S(1)} %collective-permute-done.11, f32[3,1,32,256]{3,2,1,0:T(8,128)S(1)} %collective-permute-done.10, ...), kind=kLoop, calls=%fused_computation.147 | loop fusion | flops 23592956 | bytes 4627564 | tf_op jit(solution)/shard_map/reduce_sum | solution.py:119
  285.1 63.9 %psum.31 = f32[3,1,1,1]{0,3,2,1:T(1,128)S(1)} all-reduce(f32[3,1,1,1]{0,3,2,1:T(1,128)} %bitcast.59), channel_id=1, replica_groups=mesh['bx'=4,'by'=4,'bz'=8] {'bx','by','bz'}, use_global_device_ids=true, to_apply=%region_7.8 | all-reduce | flops 3 | bytes 24 | tf_op jit(solution)/shard_map/psum | solution.py:166
  349.7 6.8 %multiply_add_fusion = (f32[3,32,32,256]{3,2,1,0:T(8,128)S(1)}, f32[3,32,32,256]{3,2,1,0:T(8,128)}, f32[3,32,32,256]{3,2,1,0:T(8,128)}) fusion(f32[3,32,32,256]{3,2,1,0:T(8,128)} %param.5, f32[3,32,32,256]{3,2,1,0:T(8,128)} %param.6, f32[3]{0:T(128)S(1)} %divide_bitcast_fusion, f32[1,32,32,256]{3,2,1,0:T(8,128)} %copy-done.4, ...), kind=kLoop, calls=%fused_computation.189 | loop fusion | flops 10223616 | bytes 22020132 | tf_op jit(solution)/shard_map/add | solution.py:177
  360.3 3.7 collective-permute-done.16
  365.6 4.0 collective-permute-start.17
  374.2 3.1 copy.78
  378.9 5.4 collective-permute-start.20
  392.2 14.2 %fusion.57 = f32[3,32,32,256]{3,2,1,0:T(8,128)S(1)} fusion(f32[3,32,32,256]{3,2,1,0:T(8,128)} %copy-done.3, f32[3,34,34,1]{3,2,1,0:T(8,128)} %copy.81, f32[3,34,1,256]{3,2,1,0:T(1,128)S(1)} %copy.75, f32[3,34,1,256]{3,2,1,0:T(1,128)S(1)} %copy.73, f32[3,1,32,256]{3,2,1,0:T(8,128)S(1)} %collective-permute-done.16, ...), kind=kLoop, calls=%fused_computation.119 | loop fusion | flops 21233664 | bytes 7773280 | tf_op jit(solution)/shard_map/add | solution.py:153
  416.1 4.7 collective-permute-start.23
  422.2 4.3 collective-permute-done.34
  435.3 5.6 collective-permute-start.26
  440.9 3.8 collective-permute-start.25
  444.7 2.9 pad_maximum_fusion.113
  452.0 3.6 collective-permute-done.35
  462.1 14.5 %fusion.48 = f32[3,32,32,256]{3,2,1,0:T(8,128)S(1)} fusion(f32[3,32,32,256]{3,2,1,0:T(8,128)} %copy-done.6, f32[3,34,34,1]{3,2,1,0:T(8,128)} %copy.91, f32[3,34,1,256]{3,2,1,0:T(1,128)S(1)} %copy.85, f32[3,34,1,256]{3,2,1,0:T(1,128)S(1)} %copy.83, f32[3,1,32,256]{3,2,1,0:T(8,128)S(1)} %collective-permute-done.22, ...), kind=kLoop, calls=%fused_computation.92 | loop fusion | flops 21233664 | bytes 7773280 | tf_op jit(solution)/shard_map/add | solution.py:153
  476.6 3.2 collective-permute-start.27
  481.2 4.7 select_maximum_fusion
  487.4 4.7 collective-permute-start.29
  498.2 3.1 copy.98
  501.3 3.1 copy.100
  506.4 3.6 collective-permute-start.31
  510.0 20.4 %fusion.119 = f32[1,32,32,256]{3,2,1,0:T(8,128)} fusion(f32[32,32,256]{2,1,0:T(8,128)S(1)} %copy-done, f32[32,32,256]{2,1,0:T(8,128)} %param.8, f32[34,34,258]{2,1,0:T(8,128)} %get-tuple-element.39, f32[34,34,258]{2,1,0:T(8,128)} %get-tuple-element.38, f32[34,34,258]{2,1,0:T(8,128)S(1)} %get-tuple-element.37), kind=kLoop, calls=%fused_computation.292 | loop fusion | flops 8126464 | bytes 28311552 | tf_op jit(solution)/shard_map/broadcast_in_dim | solution.py:183
  530.4 3.0 copy.99
  533.4 3.0 copy.101
  536.4 16.5 %fusion.127 = (f32[3,32,32,256]{3,2,1,0:T(8,128)S(1)}, f32[3,32,32,256]{3,2,1,0:T(8,128)}) fusion(f32[3,32,32,256]{3,2,1,0:T(8,128)} %copy-done.3, f32[3,32,32,256]{3,2,1,0:T(8,128)} %copy-done.7, f32[3,34,34,1]{3,2,1,0:T(8,128)} %copy.101, f32[3,34,1,256]{3,2,1,0:T(1,128)S(1)} %copy.95, f32[3,1,32,256]{3,2,1,0:T(8,128)S(1)} %collective-permute-done.28, ...), kind=kLoop, calls=%fused_computation.365 | loop fusion | flops 22020096 | bytes 14064736 | tf_op jit(solution)/shard_map/sub | solution.py:183
  552.9 4.0 collective-permute-start.36
  560.8 4.1 collective-permute-done.37
  565.2 3.4 collective-permute-start.38
  571.8 3.8 collective-permute-done.39
  577.2 3.9 fusion.130
  581.1 3.5 copy.107
  584.5 3.6 collective-permute-start.41
  588.1 3.5 copy.106
  593.7 3.5 copy.109
  597.2 3.5 copy.108
  600.7 16.1 %pad_maximum_fusion = f32[5,34,34,258]{3,2,1,0:T(8,128)S(1)} fusion(f32[5,34,34,1]{3,2,1,0:T(8,128)} %copy.109, f32[5,34,1,256]{3,2,1,0:T(1,128)} %copy-done.19, f32[5,1,32,256]{3,2,1,0:T(8,128)S(1)} %collective-permute-done.37, f32[1,32,32,256]{3,2,1,0:T(8,128)} %fusion.119, f32[1,32,32,256]{3,2,1,0:T(8,128)} %bitcast.46, ...), kind=kLoop, calls=%fused_computation | loop fusion | flops 11929920 | bytes 11929920 | tf_op jit(solution)/shard_map/concatenate | solution.py:30
  617.2 3.7 broadcast_compare_fusion.5
  621.0 6.0 broadcast_compare_fusion.1
  627.1 9.3 %fusion.84 = f32[2,32,32,256]{3,2,1,0:T(8,128)S(1)} fusion(f32[3,32,32,256]{3,2,1,0:T(8,128)S(1)} %get-tuple-element.26, f32[1,32,32,256]{3,2,1,0:T(8,128)S(1)} %bitcast.52, f32[5,34,34,1]{3,2,1,0:T(8,128)S(1)} %copy-done.13, f32[5,34,1,256]{3,2,1,0:T(1,128)S(1)} %copy-done.20, f32[5,34,1,256]{3,2,1,0:T(1,128)S(1)} %copy-done.18, ...), kind=kLoop, calls=%fused_computation.206 | loop fusion | flops 25690112 | bytes 15926432 | tf_op jit(solution)/shard_map/sub | solution.py:114
  (173 shorter events, 113.0 us)
Async XLA Ops:
  0.6 12.5 %copy-start.14 = (f32[32,32,256]{2,1,0:T(8,128)S(1)}, f32[32,32,256]{2,1,0:T(8,128)}, u32[]{:S(2)}) copy-start(f32[32,32,256]{2,1,0:T(8,128)} %param.8) | copy-start | bytes 3145732
  0.6 12.5 %copy-start = (f32[32,32,256]{2,1,0:T(8,128)S(1)}, f32[32,32,256]{2,1,0:T(8,128)}, u32[]{:S(2)}) copy-start(f32[32,32,256]{2,1,0:T(8,128)} %param.7) | copy-start | bytes 3145732
  1.6 5.3 collective-permute-start
  8.0 4.5 collective-permute-start.1
  14.1 6.8 %collective-permute-start.2 = (f32[2,33,33,1]{2,0,3,1:T(2,128)S(1)}, f32[2,33,33,1]{2,0,3,1:T(2,128)}, u32[]{:S(2)}, u32[]{:S(2)}) collective-permute-start(f32[2,33,33,1]{2,0,3,1:T(2,128)S(1)} %copy.62), channel_id=1, source_target_pairs={{0,1},{1,2},{2,3},{3,4},{4,5},{5,6},{6,7},{8,9},{9,10},{10,11},{11... | collective-permute-start | bytes 26144 | tf_op jit(solution)/shard_map/ppermute | solution.py:18
  28.7 21.6 %copy-start.4 = (f32[1,32,32,256]{3,2,1,0:T(8,128)}, f32[1,32,32,256]{3,2,1,0:T(8,128)S(1)}, u32[]{:S(2)}) copy-start(f32[1,32,32,256]{3,2,1,0:T(8,128)S(1)} %get-tuple-element.83) | copy-start | bytes 3145732
  29.0 5.6 collective-permute-start.3
  33.0 5.4 collective-permute-start.4
  38.5 6.8 %collective-permute-start.5 = (f32[3,34,1,256]{3,2,1,0:T(1,128)S(1)}, f32[3,34,1,256]{3,2,1,0:T(1,128)S(1)}, u32[]{:S(2)}, u32[]{:S(2)}) collective-permute-start(f32[3,34,1,256]{3,2,1,0:T(1,128)S(1)} %get-tuple-element.62), channel_id=1, source_target_pairs={{0,8},{8,16},{16,24},{1,9},{9,17},{17,25},{2,10},{10,18},{18,26},{... | collective-permute-start | bytes 313352 | tf_op jit(solution)/shard_map/ppermute | solution.py:26
  42.5 6.8 %collective-permute-start.6 = (f32[3,34,1,256]{3,2,1,0:T(1,128)S(1)}, f32[3,34,1,256]{3,2,1,0:T(1,128)S(1)}, u32[]{:S(2)}, u32[]{:S(2)}) collective-permute-start(f32[3,34,1,256]{3,2,1,0:T(1,128)S(1)} %get-tuple-element.63), channel_id=1, source_target_pairs={{8,0},{16,8},{24,16},{9,1},{17,9},{25,17},{10,2},{18,10},{26,18},{... | collective-permute-start | bytes 313352 | tf_op jit(solution)/shard_map/ppermute | solution.py:29
  58.9 18.8 %collective-permute-start.8 = (f32[3,34,34,1]{2,3,1,0:T(1,128)}, f32[3,34,34,1]{2,3,1,0:T(1,128)}, u32[]{:S(2)}, u32[]{:S(2)}) collective-permute-start(f32[3,34,34,1]{2,3,1,0:T(1,128)} %copy.66), channel_id=1, source_target_pairs={{1,0},{2,1},{3,2},{4,3},{5,4},{6,5},{7,6},{9,8},{10,9},{11,10},{12... | collective-permute-start | bytes 41624 | tf_op jit(solution)/shard_map/ppermute | solution.py:29
  61.2 13.6 %collective-permute-start.7 = (f32[3,34,34,1]{2,3,1,0:T(1,128)}, f32[3,34,34,1]{2,3,1,0:T(1,128)}, u32[]{:S(2)}, u32[]{:S(2)}) collective-permute-start(f32[3,34,34,1]{2,3,1,0:T(1,128)} %copy.64), channel_id=1, source_target_pairs={{0,1},{1,2},{2,3},{3,4},{4,5},{5,6},{6,7},{8,9},{9,10},{10,11},{11... | collective-permute-start | bytes 41624 | tf_op jit(solution)/shard_map/ppermute | solution.py:26
  161.3 66.0 %copy-start.22 = (f32[3]{0:T(128)}, f32[3]{0:T(128)S(1)}, u32[]{:S(2)}) copy-start(f32[3]{0:T(128)S(1)} %divide_bitcast_fusion.2) | copy-start | bytes 40
  227.2 3.1 copy-start.23
  230.4 15.8 %copy-start.5 = (f32[3,32,32,256]{3,2,1,0:T(8,128)}, f32[3,32,32,256]{3,2,1,0:T(8,128)S(1)}, u32[]{:S(2)}) copy-start(f32[3,32,32,256]{3,2,1,0:T(8,128)S(1)} %multiply_add_fusion.3) | copy-start | bytes 9437188
  230.4 4.0 collective-permute-start.9
  232.8 5.4 collective-permute-start.10
  238.3 3.4 collective-permute-start.11
  240.0 5.4 collective-permute-start.12
  251.8 10.9 %collective-permute-start.13 = (f32[3,34,34,1]{2,3,1,0:T(1,128)}, f32[3,34,34,1]{2,3,1,0:T(1,128)}, u32[]{:S(2)}, u32[]{:S(2)}) collective-permute-start(f32[3,34,34,1]{2,3,1,0:T(1,128)} %copy.68), channel_id=1, source_target_pairs={{0,1},{1,2},{2,3},{3,4},{4,5},{5,6},{6,7},{8,9},{9,10},{10,11},{11... | collective-permute-start | bytes 41624 | tf_op jit(solution)/shard_map/ppermute | solution.py:26
  260.6 5.7 collective-permute-start.14
  356.5 17.7 %copy-start.3 = (f32[3,32,32,256]{3,2,1,0:T(8,128)}, f32[3,32,32,256]{3,2,1,0:T(8,128)S(1)}, u32[]{:S(2)}) copy-start(f32[3,32,32,256]{3,2,1,0:T(8,128)S(1)} %get-tuple-element.28) | copy-start | bytes 9437188
  356.5 3.8 collective-permute-start.15
  358.7 5.4 collective-permute-start.16
  364.2 5.6 collective-permute-start.18
  365.6 5.8 collective-permute-start.17
  378.9 11.1 %collective-permute-start.20 = (f32[3,34,34,1]{2,1,3,0:T(8,128)}, f32[3,34,34,1]{2,1,3,0:T(8,128)S(1)}, u32[]{:S(2)}, u32[]{:S(2)}) collective-permute-start(f32[3,34,34,1]{2,1,3,0:T(8,128)} %copy.80), channel_id=1, source_target_pairs={{1,0},{2,1},{3,2},{4,3},{5,4},{6,5},{7,6},{9,8},{10,9},{11,10},{12... | collective-permute-start | bytes 41624 | tf_op jit(solution)/shard_map/ppermute | solution.py:29
  384.3 3.5 collective-permute-start.19
  387.8 74.3 %copy-start.15 = (f32[32,32,256]{2,1,0:T(8,128)}, f32[32,32,256]{2,1,0:T(8,128)S(1)}, u32[]{:S(2)}) copy-start(f32[32,32,256]{2,1,0:T(8,128)S(1)} %subtract_multiply_fusion) | copy-start | bytes 3145732
  392.2 18.3 %copy-start.8 = (f32[3,32,32,256]{3,2,1,0:T(8,128)S(1)}, f32[3,32,32,256]{3,2,1,0:T(8,128)}, u32[]{:S(2)}) copy-start(f32[3,32,32,256]{3,2,1,0:T(8,128)} %get-tuple-element.29) | copy-start | bytes 9437188
  406.4 20.5 %copy-start.6 = (f32[3,32,32,256]{3,2,1,0:T(8,128)}, f32[3,32,32,256]{3,2,1,0:T(8,128)S(1)}, u32[]{:S(2)}) copy-start(f32[3,32,32,256]{3,2,1,0:T(8,128)S(1)} %fusion.57) | copy-start | bytes 9437188
  406.4 5.5 collective-permute-start.21
  409.2 5.4 collective-permute-start.22
  410.6 10.2 %collective-permute-start.33 = (f32[3,1,32,256]{3,2,1,0:T(8,128)S(1)}, f32[3,1,32,256]{3,2,1,0:T(8,128)S(1)}, u32[]{:S(2)}, u32[]{:S(2)}) collective-permute-start(f32[3,1,32,256]{3,2,1,0:T(8,128)S(1)} %slice.782), channel_id=1, source_target_pairs={{32,0},{64,32},{96,64},{33,1},{65,33},{97,65},{34,2},{66,34},{98,6... | collective-permute-start | bytes 294920 | tf_op jit(solution)/shard_map/ppermute | solution.py:18
  414.8 11.8 %collective-permute-start.24 = (f32[3,34,1,256]{3,1,2,0:T(8,128)S(1)}, f32[3,34,1,256]{3,1,2,0:T(8,128)S(1)}, u32[]{:S(2)}, u32[]{:S(2)}) collective-permute-start(f32[3,34,1,256]{3,1,2,0:T(8,128)S(1)} %copy.84), channel_id=1, source_target_pairs={{8,0},{16,8},{24,16},{9,1},{17,9},{25,17},{10,2},{18,10},{26,18},{... | collective-permute-start | bytes 313352 | tf_op jit(solution)/shard_map/ppermute | solution.py:29
  416.1 10.7 %collective-permute-start.23 = (f32[3,34,1,256]{3,1,2,0:T(8,128)S(1)}, f32[3,34,1,256]{3,1,2,0:T(8,128)S(1)}, u32[]{:S(2)}, u32[]{:S(2)}) collective-permute-start(f32[3,34,1,256]{3,1,2,0:T(8,128)S(1)} %copy.82), channel_id=1, source_target_pairs={{0,8},{8,16},{16,24},{1,9},{9,17},{17,25},{2,10},{10,18},{18,26},{... | collective-permute-start | bytes 313352 | tf_op jit(solution)/shard_map/ppermute | solution.py:26
  420.9 5.6 collective-permute-start.34
  435.3 24.7 %collective-permute-start.26 = (f32[3,34,34,1]{2,1,3,0:T(8,128)S(1)}, f32[3,34,34,1]{2,1,3,0:T(8,128)S(1)}, u32[]{:S(2)}, u32[]{:S(2)}) collective-permute-start(f32[3,34,34,1]{2,1,3,0:T(8,128)S(1)} %copy.90), channel_id=1, source_target_pairs={{1,0},{2,1},{3,2},{4,3},{5,4},{6,5},{7,6},{9,8},{10,9},{11,10},{12... | collective-permute-start | bytes 41624 | tf_op jit(solution)/shard_map/ppermute | solution.py:29
  440.9 16.8 %collective-permute-start.25 = (f32[3,34,34,1]{2,1,3,0:T(8,128)S(1)}, f32[3,34,34,1]{2,1,3,0:T(8,128)S(1)}, u32[]{:S(2)}, u32[]{:S(2)}) collective-permute-start(f32[3,34,34,1]{2,1,3,0:T(8,128)S(1)} %copy.88), channel_id=1, source_target_pairs={{0,1},{1,2},{2,3},{3,4},{4,5},{5,6},{6,7},{8,9},{9,10},{10,11},{11... | collective-permute-start | bytes 41624 | tf_op jit(solution)/shard_map/ppermute | solution.py:26
  450.0 5.5 collective-permute-start.35
  462.1 19.1 %copy-start.9 = (f32[3,32,32,256]{3,2,1,0:T(8,128)S(1)}, f32[3,32,32,256]{3,2,1,0:T(8,128)}, u32[]{:S(2)}) copy-start(f32[3,32,32,256]{3,2,1,0:T(8,128)} %get-tuple-element.29) | copy-start | bytes 9437188
  462.1 19.1 %copy-start.16 = (f32[3,33,33,1]{3,2,1,0:T(8,128)S(1)}, f32[3,33,33,1]{3,2,1,0:T(8,128)}, u32[]{:S(2)}) copy-start(f32[3,33,33,1]{3,2,1,0:T(8,128)} %copy.105) | copy-start | bytes 39208
  476.6 18.2 %copy-start.7 = (f32[3,32,32,256]{3,2,1,0:T(8,128)}, f32[3,32,32,256]{3,2,1,0:T(8,128)S(1)}, u32[]{:S(2)}) copy-start(f32[3,32,32,256]{3,2,1,0:T(8,128)S(1)} %fusion.48) | copy-start | bytes 9437188
  476.6 9.3 %collective-permute-start.27 = (f32[3,1,32,256]{3,2,1,0:T(8,128)S(1)}, f32[3,1,32,256]{3,2,1,0:T(8,128)S(1)}, u32[]{:S(2)}, u32[]{:S(2)}) collective-permute-start(f32[3,1,32,256]{3,2,1,0:T(8,128)S(1)} %get-tuple-element.64), channel_id=1, source_target_pairs={{0,32},{32,64},{64,96},{1,33},{33,65},{65,97},{2,34},{34,66},{66,9... | collective-permute-start | bytes 294920 | tf_op jit(solution)/shard_map/ppermute | solution.py:26
  479.9 6.0 collective-permute-start.28
  486.1 8.4 %collective-permute-start.30 = (f32[3,34,1,256]{3,1,2,0:T(8,128)S(1)}, f32[3,34,1,256]{3,1,2,0:T(8,128)S(1)}, u32[]{:S(2)}, u32[]{:S(2)}) collective-permute-start(f32[3,34,1,256]{3,1,2,0:T(8,128)S(1)} %copy.94), channel_id=1, source_target_pairs={{8,0},{16,8},{24,16},{9,1},{17,9},{25,17},{10,2},{18,10},{26,18},{... | collective-permute-start | bytes 313352 | tf_op jit(solution)/shard_map/ppermute | solution.py:29
  487.4 7.2 %collective-permute-start.29 = (f32[3,34,1,256]{3,1,2,0:T(8,128)S(1)}, f32[3,34,1,256]{3,1,2,0:T(8,128)S(1)}, u32[]{:S(2)}, u32[]{:S(2)}) collective-permute-start(f32[3,34,1,256]{3,1,2,0:T(8,128)S(1)} %copy.92), channel_id=1, source_target_pairs={{0,8},{8,16},{16,24},{1,9},{9,17},{17,25},{2,10},{10,18},{18,26},{... | collective-permute-start | bytes 313352 | tf_op jit(solution)/shard_map/ppermute | solution.py:26
  504.5 29.0 %collective-permute-start.32 = (f32[3,34,34,1]{2,1,3,0:T(8,128)}, f32[3,34,34,1]{2,1,3,0:T(8,128)}, u32[]{:S(2)}, u32[]{:S(2)}) collective-permute-start(f32[3,34,34,1]{2,1,3,0:T(8,128)} %copy.100), channel_id=1, source_target_pairs={{1,0},{2,1},{3,2},{4,3},{5,4},{6,5},{7,6},{9,8},{10,9},{11,10},{12... | collective-permute-start | bytes 41624 | tf_op jit(solution)/shard_map/ppermute | solution.py:29
  506.4 24.0 %collective-permute-start.31 = (f32[3,34,34,1]{2,1,3,0:T(8,128)}, f32[3,34,34,1]{2,1,3,0:T(8,128)}, u32[]{:S(2)}, u32[]{:S(2)}) collective-permute-start(f32[3,34,34,1]{2,1,3,0:T(8,128)} %copy.98), channel_id=1, source_target_pairs={{0,1},{1,2},{2,3},{3,4},{4,5},{5,6},{6,7},{8,9},{9,10},{10,11},{11... | collective-permute-start | bytes 41624 | tf_op jit(solution)/shard_map/ppermute | solution.py:26
  536.4 16.5 %copy-start.1 = (f32[32,32,256]{2,1,0:T(8,128)S(1)}, f32[32,32,256]{2,1,0:T(8,128)}, u32[]{:S(2)}) copy-start(f32[32,32,256]{2,1,0:T(8,128)} %param.7) | copy-start | bytes 3145732
  536.4 16.5 %copy-start.10 = (f32[1,32,32,256]{3,2,1,0:T(8,128)S(1)}, f32[1,32,32,256]{3,2,1,0:T(8,128)}, u32[]{:S(2)}) copy-start(f32[1,32,32,256]{3,2,1,0:T(8,128)} %fusion.119) | copy-start | bytes 3145732
  552.9 7.9 %collective-permute-start.36 = (f32[5,1,32,256]{3,2,1,0:T(8,128)S(1)}, f32[5,1,32,256]{3,2,1,0:T(8,128)S(1)}, u32[]{:S(2)}, u32[]{:S(2)}) collective-permute-start(f32[5,1,32,256]{3,2,1,0:T(8,128)S(1)} %get-tuple-element.42), channel_id=1, source_target_pairs={{0,32},{32,64},{64,96},{1,33},{33,65},{65,97},{2,34},{34,66},{66,9... | collective-permute-start | bytes 491528 | tf_op jit(solution)/shard_map/ppermute | solution.py:26
  556.9 8.0 %collective-permute-start.37 = (f32[5,1,32,256]{3,2,1,0:T(8,128)S(1)}, f32[5,1,32,256]{3,2,1,0:T(8,128)S(1)}, u32[]{:S(2)}, u32[]{:S(2)}) collective-permute-start(f32[5,1,32,256]{3,2,1,0:T(8,128)S(1)} %get-tuple-element.43), channel_id=1, source_target_pairs={{32,0},{64,32},{96,64},{33,1},{65,33},{97,65},{34,2},{66,34},{98,6... | collective-permute-start | bytes 491528 | tf_op jit(solution)/shard_map/ppermute | solution.py:29
  565.2 6.6 %collective-permute-start.38 = (f32[5,34,1,256]{3,2,1,0:T(1,128)S(1)}, f32[5,34,1,256]{3,2,1,0:T(1,128)S(1)}, u32[]{:S(2)}, u32[]{:S(2)}) collective-permute-start(f32[5,34,1,256]{3,2,1,0:T(1,128)S(1)} %get-tuple-element.40), channel_id=1, source_target_pairs={{0,8},{8,16},{16,24},{1,9},{9,17},{17,25},{2,10},{10,18},{18,26},{... | collective-permute-start | bytes 522248 | tf_op jit(solution)/shard_map/ppermute | solution.py:26
  568.5 7.1 %collective-permute-start.39 = (f32[5,34,1,256]{3,2,1,0:T(1,128)S(1)}, f32[5,34,1,256]{3,2,1,0:T(1,128)S(1)}, u32[]{:S(2)}, u32[]{:S(2)}) collective-permute-start(f32[5,34,1,256]{3,2,1,0:T(1,128)S(1)} %get-tuple-element.41), channel_id=1, source_target_pairs={{8,0},{16,8},{24,16},{9,1},{17,9},{25,17},{10,2},{18,10},{26,18},{... | collective-permute-start | bytes 522248 | tf_op jit(solution)/shard_map/ppermute | solution.py:29
  571.8 5.4 copy-start.17
  584.5 9.2 %collective-permute-start.41 = (f32[5,34,34,1]{2,3,1,0:T(1,128)}, f32[5,34,34,1]{2,3,1,0:T(1,128)}, u32[]{:S(2)}, u32[]{:S(2)}) collective-permute-start(f32[5,34,34,1]{2,3,1,0:T(1,128)} %copy.107), channel_id=1, source_target_pairs={{1,0},{2,1},{3,2},{4,3},{5,4},{6,5},{7,6},{9,8},{10,9},{11,10},{12... | collective-permute-start | bytes 69368 | tf_op jit(solution)/shard_map/ppermute | solution.py:29
  591.6 5.6 collective-permute-start.40
  621.0 6.0 copy-start.2
  621.0 6.0 copy-start.11
  621.0 6.0 copy-start.12
  621.0 6.1 copy-start.13
  621.0 6.1 copy-start.18
  621.0 6.1 copy-start.20
  (3 other events, 5.3 us)
where the time goes:
time: 647 us; the launch traced here: 638 us
  blocking collectives  192 us (30%)
  other arithmetic  178 us (28%)
  starting transfers between devices  118 us (18%)
  local copies, waits for them, and re-layouts  98.8 us (15%)
  waiting for transfers between devices  49.5 us (8%)
    psum x2, blocking collectives, squares(): return lax.psum(inner(residual, residual), ('bx', 'by', 'bz'))  128 us
    ppermute x18, starting transfers between devices, padded(): lax.ppermute(lax.slice_in_dim(block, block.shape[dim] - width, None, axis...  64.5 us
    psum x1, blocking collectives, on_device(): alpha = norm_now / lax.psum(inner(direction, image), ('bx', 'by', 'bz'))  63.9 us
    ppermute x18, starting transfers between devices, padded(): lax.ppermute(lax.slice_in_dim(block, 0, width, axis=dim), axis, backward)  36.5 us
    reduce_sum x3, other arithmetic, inner(): return jnp.sum(first * second, axis=(1, 2, 3), keepdims=True)  34.7 us
    slice x19, local copies, waits for them, and re-layouts, padded(): lax.slice_in_dim(block, block.shape[dim] - width, None, axis=dim)  30.9 us
    ppermute x18, waiting for transfers between devices, padded(): lax.ppermute(lax.slice_in_dim(block, 0, width, axis=dim), axis, backward)  30.7 us
    add x2, other arithmetic, one_sweep(): return relaxed + RELAX_RATE * free * (neighbours(extended) / 6.0 - relaxed)  28.6 us
  transfers between devices with their start and end apart: 42, of which 22 were waited for; matrix products, arithmetic and copies ran while one was open for 11% of the time, Pallas kernels for 0%

commit v1 on v0

v1 whole, which is shorter than its diff:
```python
import jax
import jax.numpy as jnp
from jax import lax
from jax.experimental import pallas as pl
from jax.experimental.pallas import tpu as pltpu
from jax.sharding import PartitionSpec as P

MESH = pl.DeviceIdType.MESH
F32 = jnp.float32
N = 32
LANES = 128
PX = N + 2
PY = 48
ROWS = pl.ds(8, N)
BELOW = pl.ds(7, N)
ABOVE = pl.ds(9, N)

S_P, S_RHO, S_W, S_R, S_Q, S_ONE, S_TWO, S_VEL, S_SH, S_DE = 0, 1, 2, 5, 8, 11, 14, 17, 20, 23
SLOTS = 24
E_P, E_RHO, E_VEL, E_SH = 0, 1, 2, 5
EDGES = 8


def kernel(
    sizes,
    pos_in, vel_in, rho_in, en_in, pin_in,
    v_out, a_out, r_out, d_out, e_out,
    cell, en, vel, w, r, q, nw, nr, nq, pin, free, mass, acc, one, two, de,
    ys, yr, zs, zr, exy, exz, eyz, exyz, ze, gy, mom, ar1, ar2,
    in_sem, out_sem, face_s, face_r, edge_s, edge_r, a1s, a1r, a2s, a2r,
):
    names = ("bx", "by", "bz")
    here = [lax.axis_index(name) for name in names]
    sh = q

    def exists(step):
        ok = None
        for i in range(3):
            if step[i] == 0:
                continue
            one_ok = here[i] + step[i] >= 0 if step[i] < 0 else here[i] + step[i] < sizes[i]
            ok = one_ok if ok is None else jnp.logical_and(ok, one_ok)
        return ok

    def device(step):
        return tuple(lax.rem(here[i] + step[i] + sizes[i], sizes[i]) for i in range(3))

    def flag(step):
        return exists(step).astype(jnp.int32) > 0

    def neg(step):
        return tuple(-s for s in step)

    steps = ((-1, 0, 0), (1, 0, 0), (0, -1, 0), (0, 1, 0), (0, 0, -1), (0, 0, 1))
    lane = lax.broadcasted_iota(jnp.int32, (N, LANES), 1)
    first_lane = lane == 0
    last_lane = lane == LANES - 1

    def face_copy(slot, field, d):
        if d < 2:
            src, dst = ((1, PX - 1), (N, 0))[d]
            src, dst = field.at[:, src, ROWS, :], field.at[:, dst, ROWS, :]
        elif d < 4:
            src, dst = ys.at[slot, d - 2], yr.at[slot, 3 - d]
        else:
            src, dst = zs.at[slot, d - 4], zr.at[slot, 5 - d]
        return pltpu.make_async_remote_copy(
            src_ref=src, dst_ref=dst, send_sem=face_s.at[slot, d], recv_sem=face_r.at[slot, d],
            device_id=device(steps[d]), device_id_type=MESH)

    def edge_copies(slot, eslot, sign):
        side = 1 if sign > 0 else 0
        row = N - 1 if sign > 0 else 0
        tile = pl.ds(N - 8, 8) if sign > 0 else pl.ds(0, 8)
        pieces = (
            ((sign, sign, 0), ys.at[slot, side, :, row], exy.at[eslot]),
            ((sign, 0, sign), zs.at[slot, side], exz.at[eslot]),
            ((0, sign, sign), zs.at[slot, side, tile], eyz.at[eslot]),
            ((sign, sign, sign), zs.at[slot, side, tile], exyz.at[eslot]),
        )
        return [
            (step, pltpu.make_async_remote_copy(
                src_ref=src, dst_ref=dst, send_sem=edge_s.at[eslot, i], recv_sem=edge_r.at[eslot, i],
                device_id=device(step), device_id_type=MESH))
            for i, (step, src, dst) in enumerate(pieces)
        ]

    sent = {}

    def drain(slot):
        for step, copy in sent.pop(slot):
            pl.when(exists(step))(copy.wait_send)

    def send_faces(slot, field, ds=(0, 1, 2, 3, 4, 5)):
        for d in ds:
            copy = face_copy(slot, field, d)
            pl.when(exists(steps[d]))(copy.start)
            sent.setdefault(slot, []).append((steps[d], copy))

    def send_edges(slot, eslot, sign):
        for step, copy in edge_copies(slot, eslot, sign):
            pl.when(exists(step))(copy.start)
            sent.setdefault(slot, []).append((step, copy))

    def wait_faces(slot, field, ds=(0, 1, 2, 3, 4, 5)):
        for d in ds:
            pl.when(exists(neg(steps[d])))(face_copy(slot, field, d).wait_recv)

    def wait_edges(slot, eslot, sign):
        for step, copy in edge_copies(slot, eslot, sign):
            pl.when(exists(neg(step)))(copy.wait_recv)

    def pack_rows(slot, h, x, low, high, sides=(0, 1)):
        if 0 in sides:
            ys[slot, 0, h, x] = low
        if 1 in sides:
            ys[slot, 1, h, x] = high

    def put_low(z, a, x):
        return jnp.where(lane == x + 1, pltpu.roll(a, x + 1, 1), z)

    def put_high(z, b, x):
        return jnp.where(lane == x + 1, pltpu.roll(b, x + 2, 1), z)

    zero_plane = jnp.zeros((N, LANES), F32)

    def pack(slot, field, sides=(0, 1)):
        def body(x, zz):
            low, high = zz
            for h in range(2):
                for s in sides:
                    row = 8 if s == 0 else 7 + N
                    ys[slot, s, h, x] = field[h, x + 1, row:row + 1, :]
            if 0 in sides:
                low = put_low(low, field[0, x + 1, ROWS, :], x)
            if 1 in sides:
                high = put_high(high, field[1, x + 1, ROWS, :], x)
            return low, high
        low, high = lax.fori_loop(0, N, body, (zero_plane, zero_plane), unroll=2)
        if 0 in sides:
            zs[slot, 0] = low
        if 1 in sides:
            zs[slot, 1] = high

    def unpack_rows(slot, field, sides=(0, 1)):
        have = [flag((0, -1, 0)), flag((0, 1, 0))]

        def body(x, _):
            for s in sides:
                row = 7 if s == 0 else 8 + N
                for h in range(2):
                    got = yr[slot, s, h, x]
                    field[h, x + 1, row:row + 1, :] = jnp.where(have[s], got, jnp.zeros_like(got))
            return 0
        lax.fori_loop(0, N, body, 0, unroll=4)

    def z_halo(slot, side):
        have = flag((0, 0, -1 if side == 0 else 1))
        return jnp.where(have, zr[slot, side], zero_plane)

    def edge_halo(slot, eslot, field, sign):
        side = 0 if sign > 0 else 1
        unpack_rows(slot, field, (side,))
        step = -sign
        plane, row = (0, 7) if sign > 0 else (PX - 1, 8 + N)
        have = flag((step, step, 0))
        for h in range(2):
            got = exy[eslot, h]
            field[h, plane, row:row + 1, :] = jnp.where(have, got, jnp.zeros_like(got))
        turn, at = (LANES - N, 0) if sign > 0 else (N, N + 1)
        beside = jnp.where(flag((step, 0, step)), exz[eslot], zero_plane)
        ze[eslot, ROWS, :] = jnp.where(lane == at, pltpu.roll(beside, turn, 1), z_halo(slot, side))
        tile_lane = lax.broadcasted_iota(jnp.int32, (8, LANES), 1)
        zero_tile = jnp.zeros((8, LANES), F32)
        corner = jnp.where(flag((step, step, step)), exyz[eslot], zero_tile)
        across = jnp.where(flag((0, step, step)), eyz[eslot], zero_tile)
        tile = pl.ds(0, 8) if sign > 0 else pl.ds(8 + N, 8)
        ze[eslot, tile, :] = jnp.where(tile_lane == at, pltpu.roll(corner, turn, 1), across)

    def clear_missing(field, planes=(0, PX - 1)):
        for plane in planes:
            step = (-1, 0, 0) if plane == 0 else (1, 0, 0)

            @pl.when(jnp.logical_not(exists(step)))
            def _():
                for h in range(2):
                    field[h, plane, ROWS, :] = zero_plane

    def z_below(a, b, halo):
        ra, rb = pltpu.roll(a, 1, 1), pltpu.roll(b, 1, 1)
        return jnp.where(first_lane, halo, ra), jnp.where(first_lane, ra, rb)

    def z_above(a, b, halo):
        ra, rb = pltpu.roll(a, LANES - 1, 1), pltpu.roll(b, LANES - 1, 1)
        return jnp.where(last_lane, rb, ra), jnp.where(last_lane, halo, rb)

    def to_first(z, at):
        return pltpu.roll(z, lax.rem(LANES - at, LANES), 1)

    def to_last(z, at):
        return pltpu.roll(z, LANES - 1 - at, 1)

    def neighbours(field, x, low, high):
        i = x + 1
        a, b = field[0, i, ROWS, :], field[1, i, ROWS, :]
        am, bm = z_below(a, b, to_first(low, i))
        ap, bp = z_above(a, b, to_last(high, i))
        out = []
        for h, (m, p) in enumerate(((am, ap), (bm, bp))):
            s = (field[h, i - 1, ROWS, :] + field[h, i + 1, ROWS, :]) + (
                field[h, i, BELOW, :] + field[h, i, ABOVE, :])
            out.append(s + (m + p))
        return (a, b), out

    def fold(v):
        return (v[0:8] + v[8:16]) + (v[16:24] + v[24:32])

    def halves(k):
        return pl.ds(k * LANES, LANES)

    loads = {}
    for h in range(2):
        loads["rho", h] = pltpu.make_async_copy(
            rho_in.at[:, :, halves(h)], cell.at[1, h, pl.ds(1, N), ROWS, :], in_sem.at[0, h])
        loads["en", h] = pltpu.make_async_copy(en_in.at[:, :, halves(h)], en.at[h], in_sem.at[1, h])
        loads["vel", h] = pltpu.make_async_copy(
            vel_in.at[:, :, :, halves(h)], vel.at[:, h, pl.ds(1, N), ROWS, :], in_sem.at[2, h])
        loads["pos", h] = pltpu.make_async_copy(
            pos_in.at[:, :, :, halves(h)], w.at[:, h, pl.ds(1, N), ROWS, :], in_sem.at[3, h])
        loads["pin", h] = pltpu.make_async_copy(pin_in.at[:, :, halves(h)], pin.at[h], in_sem.at[4, h])
    for name in ("rho", "en", "vel", "pos", "pin"):
        for h in range(2):
            loads[name, h].start()

    clear_missing(cell.at[0], (0,))
    clear_missing(cell.at[1])
    clear_missing(de)
    for c in range(3):
        for field in (w, r, q, one, two):
            clear_missing(field.at[c])
        clear_missing(vel.at[c], (PX - 1,))

    barrier = pltpu.get_barrier_semaphore()
    around = [s for s in ((i, j, k) for i in (0, 1) for j in (0, 1) for k in (0, 1)) if any(s)]
    around = around + [neg(s) for s in around]
    count = 0
    for step in around:
        @pl.when(exists(step))
        def _():
            pl.semaphore_signal(barrier, inc=1, device_id=device(step), device_id_type=MESH)
        count = count + exists(step).astype(jnp.int32)
    nz, nxy = sizes[2], sizes[0] * sizes[1]

    def z_peer(k):
        return (here[0], here[1], lax.rem(here[2] + k, nz))

    def xy_peer(k):
        return (lax.rem(here[0] + k // sizes[1], sizes[0]), lax.rem(here[1] + k % sizes[1], sizes[1]), here[2])

    for k in range(1, nz):
        pl.semaphore_signal(barrier, inc=1, device_id=z_peer(k), device_id_type=MESH)
    for k in range(1, nxy):
        pl.semaphore_signal(barrier, inc=1, device_id=xy_peer(k), device_id_type=MESH)

    for name in ("rho", "en"):
        for h in range(2):
            loads[name, h].wait()

    def pressure_body(x, zz):
        ph, rl, rh = zz
        for h in range(2):
            rho = cell[1, h, x + 1, ROWS, :]
            p = 0.1 * rho * en[h, x]
            cell[0, h, x + 1, ROWS, :] = p
            ys[S_P, 1, h, x] = p[N - 1:N]
            ys[S_RHO, 0, h, x] = rho[0:1]
            ys[S_RHO, 1, h, x] = rho[N - 1:N]
            if h == 0:
                rl = put_low(rl, rho, x)
            else:
                ph = put_high(ph, p, x)
                rh = put_high(rh, rho, x)
        return ph, rl, rh

    ph, rl, rh = lax.fori_loop(0, N, pressure_body, (zero_plane,) * 3)
    zs[S_P, 1] = ph
    zs[S_RHO, 0] = rl
    zs[S_RHO, 1] = rh

    pl.semaphore_wait(barrier, count + (nz - 1) + (nxy - 1))
    send_edges(S_P, E_P, 1)
    send_edges(S_RHO, E_RHO, 1)
    send_faces(S_P, cell.at[0], (5, 3, 1))
    send_faces(S_RHO, cell.at[1], (5, 3, 1, 4, 2, 0))

    for name in ("vel", "pos", "pin"):
        for h in range(2):
            loads[name, h].wait()

    def advance(c):
        def body(x, zz):
            low, high = zz
            for h in range(2):
                v = w[c, h, x + 1, ROWS, :] + 0.6 * vel[c, h, x + 1, ROWS, :]
                w[c, h, x + 1, ROWS, :] = v
                pack_rows(S_W + c, h, x, v[0:1], v[N - 1:N])
                if h == 0:
                    low = put_low(low, v, x)
                else:
                    high = put_high(high, v, x)
            return low, high
        low, high = lax.fori_loop(0, N, body, (zero_plane,) * 2)
        zs[S_W + c, 0] = low
        zs[S_W + c, 1] = high
        send_faces(S_W + c, w.at[c])

    for c in range(3):
        advance(c)

    def mask_body(x, _):
        for h in range(2):
            free[h, x] = 0.8 - 0.8 * pin[h, x].astype(F32)
        return 0
    lax.fori_loop(0, N, mask_body, 0)

    wait_faces(S_P, cell.at[0], (5, 3, 1))
    wait_edges(S_P, E_P, 1)
    wait_faces(S_RHO, cell.at[1])
    wait_edges(S_RHO, E_RHO, 1)
    edge_halo(S_P, E_P, cell.at[0], 1)
    edge_halo(S_RHO, E_RHO, cell.at[1], 1)
    unpack_rows(S_RHO, cell.at[1], (1,))
    zay = ze[E_P, ROWS, :] + ze[E_P, BELOW, :]
    zdy = ze[E_P, BELOW, :] - ze[E_P, ROWS, :]
    zrho = ze[E_RHO, ROWS, :] + ze[E_RHO, BELOW, :]

    def force_terms(i):
        ay, dy = [], []
        for h in range(2):
            c, b = cell[0, h, i, ROWS, :], cell[0, h, i, BELOW, :]
            ay.append(c + b)
            dy.append(b - c)
        aym = z_below(ay[0], ay[1], to_first(zay, i))
        dym = z_below(dy[0], dy[1], to_first(zdy, i))
        return tuple(
            t for h in range(2) for t in (ay[h] + aym[h], dy[h] + dym[h], aym[h] - ay[h]))

    def force_body(x, before):
        now = force_terms(x + 1)
        for h in range(2):
            r[0, h, x + 1, ROWS, :] = before[3 * h] - now[3 * h]
            r[1, h, x + 1, ROWS, :] = before[3 * h + 1] + now[3 * h + 1]
            r[2, h, x + 1, ROWS, :] = before[3 * h + 2] + now[3 * h + 2]
        return now
    lax.fori_loop(0, N, force_body, force_terms(0))

    for c in range(3):
        pack(S_R + c, r.at[c])
        send_faces(S_R + c, r.at[c])

    def mass_terms(i):
        ay = [cell[1, h, i, ROWS, :] + cell[1, h, i, BELOW, :] for h in range(2)]
        aym = z_below(ay[0], ay[1], to_first(zrho, i))
        return ay[0] + aym[0], ay[1] + aym[1]

    def mass_body(x, before):
        now = mass_terms(x + 1)
        for h in range(2):
            mass[h, x] = 0.125 * (before[h] + now[h]) + 1.2
        return now
    lax.fori_loop(0, N, mass_body, mass_terms(0))

    zero_tile = jnp.zeros((8, LANES), F32)

    def receive(slot, field):
        wait_faces(slot, field)
        unpack_rows(slot, field)
        return z_halo(slot, 0), z_halo(slot, 1)

    for c in range(3):
        zl, zh = receive(S_R + c, r.at[c])

        def image_body(x, carry, c=c, zl=zl, zh=zh):
            low, high, m0, m1, m2 = carry
            centre, near = neighbours(r.at[c], x, zl, zh)
            for h in range(2):
                image = mass[h, x] * centre[h] + 0.2 * near[h]
                q[c, h, x + 1, ROWS, :] = image
                nr[c, h, x] = near[h]
                m0 = m0 + fold(centre[h] * centre[h])
                m1 = m1 + fold(centre[h] * image)
                m2 = m2 + fold(image * image)
                pack_rows(S_Q + c, h, x, image[0:1], image[N - 1:N])
                if h == 0:
                    low = put_low(low, image, x)
                else:
                    high = put_high(high, image, x)
            return low, high, m0, m1, m2
        low, high, m0, m1, m2 = lax.fori_loop(
            0, N, image_body, (zero_plane, zero_plane, zero_tile, zero_tile, zero_tile))
        zs[S_Q + c, 0] = low
        zs[S_Q + c, 1] = high
        send_faces(S_Q + c, q.at[c])
        for k, m in enumerate((m0, m1, m2)):
            mom[4 * c + k:4 * c + k + 1, :] = jnp.sum(m, axis=0, keepdims=True)

    def near_w(c):
        zl, zh = receive(S_W + c, w.at[c])

        def body(x, _):
            _c, near = neighbours(w.at[c], x, zl, zh)
            for h in range(2):
                nw[c, h, x] = near[h]
            return 0
        lax.fori_loop(0, N, body, 0)

    near_w(0)
    for c in range(3):
        zl, zh = receive(S_Q + c, q.at[c])

        def second_body(x, m3, c=c, zl=zl, zh=zh):
            centre, near = neighbours(q.at[c], x, zl, zh)
            for h in range(2):
                nq[c, h, x] = near[h]
                m3 = m3 + fold(centre[h] * (mass[h, x] * centre[h] + 0.2 * near[h]))
            return m3
        m3 = lax.fori_loop(0, N, second_body, zero_tile)
        mom[4 * c + 3:4 * c + 4, :] = jnp.sum(m3, axis=0, keepdims=True)
    mom[12:16, :] = jnp.zeros((4, LANES), F32)

    total = jnp.sum(mom[...], axis=1, keepdims=True)
    on_row = lax.broadcasted_iota(jnp.int32, (16, LANES), 0)
    on_lane = lax.broadcasted_iota(jnp.int32, (16, LANES), 1)
    ar1[0] = jnp.sum(jnp.where(on_row == on_lane, total, 0.0), axis=0, keepdims=True)

    def reduce_copies(buf, send, recv, peer, peers):
        return [
            pltpu.make_async_remote_copy(
                src_ref=buf.at[0], dst_ref=buf.at[k], send_sem=send.at[k], recv_sem=recv.at[k],
                device_id=peer(k), device_id_type=MESH)
            for k in range(1, peers)
        ]

    def gathered(buf, copies):
        for copy in copies:
            copy.wait_recv()
        parts = [buf[k] for k in range(len(copies) + 1)]
        while len(parts) > 1:
            parts = [a + b for a, b in zip(parts[::2], parts[1::2])]
        return parts[0]

    along = reduce_copies(ar1, a1s, a1r, z_peer, nz)
    for copy in along:
        copy.start()
    near_w(1)
    ar2[0] = gathered(ar1, along)
    across = reduce_copies(ar2, a2s, a2r, xy_peer, nxy)
    for copy in across:
        copy.start()
    near_w(2)
    sums = gathered(ar2, across)
    row_lane = lax.broadcasted_iota(jnp.int32, (1, LANES), 1)

    def pick(k):
        return jnp.sum(jnp.where(row_lane == k, sums, 0.0), axis=1, keepdims=True)

    outs = []

    def write(src, dst, i, h):
        copy = pltpu.make_async_copy(src, dst, out_sem.at[i, h])
        copy.start()
        outs.append(copy)

    for c in range(3):
        m0, m1, m2, m3 = [pick(4 * c + k) for k in range(4)]
        a1 = m0 / m1
        new = m0 - 2.0 * a1 * m1 + a1 * a1 * m2
        b1 = 1.0 + new / m0
        a2 = new / (b1 * b1 * m1 - 2.0 * a1 * b1 * m2 + a1 * a1 * m3)
        c1 = jnp.broadcast_to(a1 + a2 * b1, (N, LANES))
        c2 = jnp.broadcast_to(-a1 * a2, (N, LANES))

        def step_body(x, carry, c=c, c1=c1, c2=c2):
            low, high = carry
            i = x + 1
            for h in range(2):
                a = c1 * r[c, h, i, ROWS, :] + c2 * q[c, h, i, ROWS, :]
                acc[c, h, x] = a
                v = vel[c, h, i, ROWS, :] + 0.6 * a
                vel[c, h, i, ROWS, :] = v
                moved = w[c, h, i, ROWS, :] + 0.36 * a
                w[c, h, i, ROWS, :] = moved
                near = nw[c, h, x] + 0.36 * (c1 * nr[c, h, x] + c2 * nq[c, h, x])
                u = moved + free[h, x] * (near * (1.0 / 6.0) - moved)
                one[c, h, i, ROWS, :] = u
                pack_rows(S_ONE + c, h, x, u[0:1], u[N - 1:N])
                if h == 0:
                    low = put_low(low, u, x)
                else:
                    high = put_high(high, u, x)
            return low, high
        drain(S_W + c)
        low, high = lax.fori_loop(0, N, step_body, (zero_plane,) * 2)
        zs[S_ONE + c, 0] = low
        zs[S_ONE + c, 1] = high
        send_faces(S_ONE + c, one.at[c])
    for c in range(3):
        pack(S_VEL + c, vel.at[c], (0,))
        send_faces(S_VEL + c, vel.at[c], (0, 2, 4))
        send_edges(S_VEL + c, E_VEL + c, -1)
        for h in range(2):
            write(acc.at[c, h], a_out.at[c, :, :, halves(h)], c, h)
            write(vel.at[c, h, pl.ds(1, N), ROWS, :], v_out.at[c, :, :, halves(h)], 3 + c, h)

    def swept(field, c, x, zl, zh):
        centre, near = neighbours(field.at[c], x, zl, zh)
        return [centre[h] + free[h, x] * (near[h] * (1.0 / 6.0) - centre[h]) for h in range(2)]

    for c in range(3):
        zl, zh = receive(S_ONE + c, one.at[c])

        def sweep_body(x, carry, c=c, zl=zl, zh=zh):
            low, high = carry
            u = swept(one, c, x, zl, zh)
            for h in range(2):
                two[c, h, x + 1, ROWS, :] = u[h]
                pack_rows(S_TWO + c, h, x, u[h][0:1], u[h][N - 1:N])
            return put_low(low, u[0], x), put_high(high, u[1], x)
        low, high = lax.fori_loop(0, N, sweep_body, (zero_plane,) * 2)
        zs[S_TWO + c, 0] = low
        zs[S_TWO + c, 1] = high
        send_faces(S_TWO + c, two.at[c])

    for c in range(3):
        wait_faces(S_VEL + c, vel.at[c], (0, 2, 4))
        wait_edges(S_VEL + c, E_VEL + c, -1)
        edge_halo(S_VEL + c, E_VEL + c, vel.at[c], -1)

    def rows_up(k):
        return ze[k, ROWS, :], ze[k, ABOVE, :]

    zx, zy, zz3 = rows_up(E_VEL), rows_up(E_VEL + 1), rows_up(E_VEL + 2)
    z_s1 = (zy[1] - zy[0]) + (zz3[0] + zz3[1])
    z_s2 = zx[0] + zx[1]

    def div_terms(i):
        s1, s2, s3 = [], [], []
        for h in range(2):
            ax = vel[0, h, i, ROWS, :] + vel[0, h, i, ABOVE, :]
            dy = vel[1, h, i, ABOVE, :] - vel[1, h, i, ROWS, :]
            az = vel[2, h, i, ROWS, :] + vel[2, h, i, ABOVE, :]
            s1.append(dy + az)
            s2.append(ax)
            s3.append(dy - az)
        u1 = z_above(s1[0], s1[1], to_last(z_s1, i))
        u2 = z_above(s2[0], s2[1], to_last(z_s2, i))
        plus, minus = [], []
        for h in range(2):
            flat, along_x = s3[h] + u1[h], s2[h] + u2[h]
            plus.append(flat + along_x)
            minus.append(flat - along_x)
        return plus, minus

    def div_body(x, carry):
        b0, b1, low, high = carry
        plus, minus = div_terms(x + 2)
        for h, before in enumerate((b0, b1)):
            spread = before + plus[h]
            value = cell[1, h, x + 1, ROWS, :] * (en[h, x] * (1.0 - 0.06 * spread))
            de[h, x + 1, ROWS, :] = value
            pack_rows(S_DE, h, x, value[0:1], value[N - 1:N])
            if h == 0:
                low = put_low(low, value, x)
            else:
                high = put_high(high, value, x)
        return minus[0], minus[1], low, high
    _plus, minus = div_terms(1)
    _0, _1, low, high = lax.fori_loop(0, N, div_body, (minus[0], minus[1], zero_plane, zero_plane))
    zs[S_DE, 0] = low
    zs[S_DE, 1] = high
    send_faces(S_DE, de)

    for c in range(3):
        zl, zh = receive(S_TWO + c, two.at[c])

        def last_body(x, low, c=c, zl=zl, zh=zh):
            u = swept(two, c, x, zl, zh)
            for h in range(2):
                nw[c, h, x] = u[h]
                s = u[h] - w[c, h, x + 1, ROWS, :]
                sh[c, h, x + 1, ROWS, :] = s
                pack_rows(S_SH + c, h, x, s[0:1], None, (0,))
                if h == 0:
                    low = put_low(low, s, x)
            return low
        drain(S_Q + c)
        zs[S_SH + c, 0] = lax.fori_loop(0, N, last_body, zero_plane)
        send_faces(S_SH + c, sh.at[c], (4, 2, 0))
        send_edges(S_SH + c, E_SH + c, -1)
        for h in range(2):
            write(nw.at[c, h], r_out.at[c, :, :, halves(h)], 6 + c, h)

    fields = (cell.at[1], de)
    slots = (S_RHO, S_DE)
    receive(S_DE, de)
    for c in range(3):
        wait_faces(S_SH + c, sh.at[c], (4, 2, 0))
        wait_edges(S_SH + c, E_SH + c, -1)
        edge_halo(S_SH + c, E_SH + c, sh.at[c], -1)
    zx, zz3 = rows_up(E_SH), rows_up(E_SH + 2)
    z_ax = zx[0] + zx[1]
    wide = pl.ds(8, 40)
    z_y = ze[E_SH + 1, wide, :]
    z_y = z_y + pltpu.roll(z_y, LANES - 1, 1)
    z_z = zz3[0] + zz3[1]
    z_z = 0.25 * (z_z + pltpu.roll(z_z, LANES - 1, 1))
    low_q = [z_halo(slot, 0) for slot in slots]
    top_g = [z_z * jnp.where(z_z > 0, z_halo(slot, 1), zs[slot, 1]) for slot in slots]
    wide_last = lax.broadcasted_iota(jnp.int32, (40, LANES), 1) == LANES - 1

    def flux_x(i):
        a = [sh[0, h, i, ROWS, :] + sh[0, h, i, ABOVE, :] for h in range(2)]
        up = z_above(a[0], a[1], to_last(z_ax, i))
        out = []
        for h in range(2):
            s = 0.25 * (a[h] + up[h])
            for field in fields:
                out.append(s * jnp.where(s > 0, field[h, i, ROWS, :], field[h, i - 1, ROWS, :]))
        return tuple(out)

    def remap_body(x, before):
        i = x + 1
        now = flux_x(i + 1)
        t = [sh[1, h, i, wide, :] + sh[1, h, i + 1, wide, :] for h in range(2)]
        ra, rb = [pltpu.roll(v, LANES - 1, 1) for v in t]
        up = (jnp.where(wide_last, rb, ra), jnp.where(wide_last, to_last(z_y, i), rb))
        for h in range(2):
            s = 0.25 * (t[h] + up[h])
            for f, field in enumerate(fields):
                gy[f, h] = s * jnp.where(s > 0, field[h, i, wide, :], field[h, i, pl.ds(7, 40), :])
        s = [
            0.25 * ((sh[2, h, i, ROWS, :] + sh[2, h, i, ABOVE, :])
                    + (sh[2, h, i + 1, ROWS, :] + sh[2, h, i + 1, ABOVE, :]))
            for h in range(2)
        ]
        for f, field in enumerate(fields):
            own = [field[h, i, ROWS, :] for h in range(2)]
            under = z_below(own[0], own[1], to_first(low_q[f], i))
            g = [s[h] * jnp.where(s[h] > 0, own[h], under[h]) for h in range(2)]
            over = z_above(g[0], g[1], to_last(top_g[f], i))
            for h in range(2):
                nr[f, h, x] = (
                    own[h] + (now[2 * h + f] - before[2 * h + f])
                    + (gy[f, h, 1:N + 1, :] - gy[f, h, 0:N, :]) + (over[h] - g[h]))
        return now
    lax.fori_loop(0, N, remap_body, flux_x(1))
    for f, out in enumerate((d_out, e_out)):
        for h in range(2):
            write(nr.at[f, h], out.at[:, :, halves(h)], 9 + f, h)

    for slot in tuple(sent):
        drain(slot)
    for copy in along + across:
        copy.wait_send()
    for copy in outs:
        copy.wait()


def solution(mesh):
    sizes = tuple(mesh.shape[name] for name in ("bx", "by", "bz"))
    vector = P(None, "bx", "by", "bz")
    scalar = P("bx", "by", "bz")

    def on_device(position, velocity, density, energy, pinned):
        def padded(*lead):
            return pltpu.VMEM(lead + (2, PX, PY, LANES), F32)

        def plain(*lead, dtype=F32):
            return pltpu.VMEM(lead + (2, N, N, LANES), dtype)

        dma = pltpu.SemaphoreType.DMA
        v3 = jax.ShapeDtypeStruct(position.shape, F32)
        v1 = jax.ShapeDtypeStruct(density.shape, F32)
        anywhere = pl.BlockSpec(memory_space=pl.ANY)

        def body(*refs):
            kernel(sizes, *refs)

        return tuple(pl.pallas_call(
            body,
            name="lagrangian_step",
            out_shape=(v3, v3, v3, v1, v1),
            in_specs=[anywhere] * 5,
            out_specs=[anywhere] * 5,
            scratch_shapes=[
                padded(2), plain(), padded(3), padded(3), padded(3), padded(3),
                plain(3), plain(3), plain(3), plain(dtype=jnp.int32), plain(), plain(), plain(3),
                padded(3), padded(3), padded(),
                pltpu.VMEM((SLOTS, 2, 2, N, 1, LANES), F32),
                pltpu.VMEM((SLOTS, 2, 2, N, 1, LANES), F32),
                pltpu.VMEM((SLOTS, 2, N, LANES), F32),
                pltpu.VMEM((SLOTS, 2, N, LANES), F32),
                pltpu.VMEM((EDGES, 2, 1, LANES), F32),
                pltpu.VMEM((EDGES, N, LANES), F32),
                pltpu.VMEM((EDGES, 8, LANES), F32),
                pltpu.VMEM((EDGES, 8, LANES), F32),
                pltpu.VMEM((EDGES, PY, LANES), F32),
                pltpu.VMEM((2, 2, 40, LANES), F32),
                pltpu.VMEM((16, LANES), F32),
                pltpu.VMEM((sizes[2], 1, LANES), F32),
                pltpu.VMEM((sizes[0] * sizes[1], 1, LANES), F32),
                dma((5, 2)), dma((11, 2)),
                dma((SLOTS, 6)), dma((SLOTS, 6)), dma((EDGES, 4)), dma((EDGES, 4)),
                dma((sizes[2],)), dma((sizes[2],)),
                dma((sizes[0] * sizes[1],)), dma((sizes[0] * sizes[1],)),
            ],
            compiler_params=pltpu.CompilerParams(
                collective_id=0, has_side_effects=True, vmem_limit_bytes=66 * 1000 * 1000),
        )(position, velocity, density, energy, pinned))

    return jax.shard_map(
        on_device,
        mesh=mesh,
        in_specs=(vector, vector, scalar, scalar, scalar),
        out_specs=(vector, vector, vector, scalar, scalar),
        check_vma=False,
    )
```

time: 647 us -> 146 us (0.23); the launches traced: 638 us -> 145 us
  blocking collectives: 192 us -> 0 us
  other arithmetic: 178 us -> 0 us
  Pallas kernels: 0 us -> 134 us
  starting transfers between devices: 118 us -> 0 us
  local copies, waits for them, and re-layouts: 98.8 us -> 11 us
  waiting for transfers between devices: 49.5 us -> 0 us
    psum x3 -> x0, blocking collectives: 192 us -> none  [the longest x2 128 us: squares(): return lax.psum(inner(residual, residual), ('bx', 'by', 'bz'))]
    pallas_call x0 -> x1, Pallas kernels: none -> 134 us  [on_device(): pl.pallas_call(body, name='lagrangian_step', out_shape=(v3, v3, v3, v1, v...]
    ppermute x42 -> x0, starting transfers between devices: 118 us -> none  [the longest x18 64.5 us: padded(): lax.ppermute(lax.slice_in_dim(block, block.shape[dim] - width, None, axis...]
    slice x33 -> x0, local copies, waits for them, and re-layouts: 54.6 us -> none  [the longest x19 30.9 us: padded(): lax.slice_in_dim(block, block.shape[dim] - width, None, axis=dim)]
    ppermute x42 -> x0, waiting for transfers between devices: 49.5 us -> none  [the longest x18 30.7 us: padded(): lax.ppermute(lax.slice_in_dim(block, 0, width, axis=dim), axis, backward)]
    add x4 -> x0, other arithmetic: 38.5 us -> none  [the longest x2 28.6 us: one_sweep(): return relaxed + RELAX_RATE * free * (neighbours(extended) / 6.0 - relaxed)]
    ppermute x21 -> x0, local copies, waits for them, and re-layouts: 37.6 us -> none  [the longest x9 17 us: padded(): lax.ppermute(lax.slice_in_dim(block, block.shape[dim] - width, None, axis...]
    reduce_sum x3 -> x0, other arithmetic: 34.7 us -> none  [inner(): return jnp.sum(first * second, axis=(1, 2, 3), keepdims=True)]
  transfers between devices with their start and end apart: 42 -> 0, of which waited for: 22 -> 0; matrix products, arithmetic and copies ran while one was open for 11% -> 0% of each run, Pallas kernels for 0% -> 0%
where the time goes in v1:
time: 146 us; the launch traced here: 145 us
  Pallas kernels  134 us (92%)
  local copies, waits for them, and re-layouts  11 us (8%)
    pallas_call x1, Pallas kernels, on_device(): pl.pallas_call(body, name='lagrangian_step', out_shape=(v3, v3, v3, v1, v...  134 us
    unnamed x13, local copies, waits for them, and re-layouts  11 us

profile of v1, /device:TPU:1, one launch (start us, length us, event | category | flops | bytes accessed | tf_op | source)
XLA Modules:
  0.0 145.4 jit_solution(12433844317364547425)
XLA Ops:
  0.6 133.7 %lagrangian_step.1 = (f32[3,32,32,256]{3,2,1,0:T(8,128)}, f32[3,32,32,256]{3,2,1,0:T(8,128)}, f32[3,32,32,256]{3,2,1,0:T(8,128)}, f32[32,32,256]{2,1,0:T(8,128)}, f32[32,32,256]{2,1,0:T(8,128)}) custom-call(f32[3,32,32,256]{3,2,1,0:T(8,128)} %refs_0_.1, f32[3,32,32,256]{3,2,1,0:T(8,128)} %refs_1_.1, f32[32,32,256]{2,1,0:T(8,128)} %refs_2_.1, ...), custom_call_target="tpu_custom_call" | custom-call | tf_op jit(solution)/shard_map/lagrangian_step/pallas_call | solution.py:689
  134.4 0.0 copy-start.1
  134.4 4.1 %copy.15 = f32[3,32,32,256]{3,2,1,0:T(8,128)} copy(f32[3,32,32,256]{3,2,1,0:T(8,128)} %get-tuple-element.10) | data formatting | bytes 6291456
  138.5 0.0 copy-done.1
  138.5 0.0 copy-start
  138.5 1.7 %copy.16 = f32[3,32,32,256]{3,2,1,0:T(8,128)} copy(f32[3,32,32,256]{3,2,1,0:T(8,128)S(1)} %copy-done.1) | data formatting | bytes 6291456
  140.2 1.4 copy-done
  141.5 0.0 copy-start.3
  141.5 0.0 copy-start.2
  141.5 1.7 %copy.17 = f32[3,32,32,256]{3,2,1,0:T(8,128)} copy(f32[3,32,32,256]{3,2,1,0:T(8,128)S(1)} %copy-done) | data formatting | bytes 6291456
  143.2 0.3 copy-done.3
  143.5 1.0 copy.18
  144.5 0.0 copy-done.2
  144.5 1.0 copy.19
Async XLA Ops:
  134.4 4.1 %copy-start.1 = (f32[3,32,32,256]{3,2,1,0:T(8,128)S(1)}, f32[3,32,32,256]{3,2,1,0:T(8,128)}, u32[]{:S(2)}) copy-start(f32[3,32,32,256]{3,2,1,0:T(8,128)} %get-tuple-element.11) | copy-start | bytes 9437188
  138.5 3.0 %copy-start = (f32[3,32,32,256]{3,2,1,0:T(8,128)S(1)}, f32[3,32,32,256]{3,2,1,0:T(8,128)}, u32[]{:S(2)}) copy-start(f32[3,32,32,256]{3,2,1,0:T(8,128)} %get-tuple-element.12) | copy-start | bytes 9437188
  141.5 2.0 %copy-start.3 = (f32[32,32,256]{2,1,0:T(8,128)S(1)}, f32[32,32,256]{2,1,0:T(8,128)}, u32[]{:S(2)}) copy-start(f32[32,32,256]{2,1,0:T(8,128)} %get-tuple-element.13) | copy-start | bytes 3145732
  141.5 2.9 %copy-start.2 = (f32[32,32,256]{2,1,0:T(8,128)S(1)}, f32[32,32,256]{2,1,0:T(8,128)}, u32[]{:S(2)}) copy-start(f32[32,32,256]{2,1,0:T(8,128)} %get-tuple-element.14) | copy-start | bytes 3145732

commit v2 on v1

--- a/solution.py
+++ b/solution.py
@@ -63,7 +63,7 @@
         elif d < 4:
             src, dst = ys.at[slot, d - 2], yr.at[slot, 3 - d]
         else:
-            src, dst = zs.at[slot, d - 4], zr.at[slot, 5 - d]
+            src, dst = zs.at[slot], zr.at[slot, 5 - d]
         return pltpu.make_async_remote_copy(
             src_ref=src, dst_ref=dst, send_sem=face_s.at[slot, d], recv_sem=face_r.at[slot, d],
             device_id=device(steps[d]), device_id_type=MESH)
@@ -74,9 +74,9 @@
         tile = pl.ds(N - 8, 8) if sign > 0 else pl.ds(0, 8)
         pieces = (
             ((sign, sign, 0), ys.at[slot, side, :, row], exy.at[eslot]),
-            ((sign, 0, sign), zs.at[slot, side], exz.at[eslot]),
-            ((0, sign, sign), zs.at[slot, side, tile], eyz.at[eslot]),
-            ((sign, sign, sign), zs.at[slot, side, tile], exyz.at[eslot]),
+            ((sign, 0, sign), zs.at[slot], exz.at[eslot]),
+            ((0, sign, sign), zs.at[slot, tile], eyz.at[eslot]),
+            ((sign, sign, sign), zs.at[slot, tile], exyz.at[eslot]),
         )
         return [
             (step, pltpu.make_async_remote_copy(
@@ -110,37 +110,48 @@
         for step, copy in edge_copies(slot, eslot, sign):
             pl.when(exists(neg(step)))(copy.wait_recv)
 
-    def pack_rows(slot, h, x, low, high, sides=(0, 1)):
+    zero_plane = jnp.zeros((N, LANES), F32)
+    odd = lane % 2 == 1
+    left = lane < LANES // 2
+
+    def planes(body, init=0, trip=4):
+        def run(i, carry):
+            return body([i * trip + j for j in range(trip)], carry)
+        return lax.fori_loop(0, N // trip, run, init)
+
+    def lagging(xs):
+        back = jnp.minimum(xs[0], len(xs))
+        return [x - back for x in xs]
+
+    def pack_planes(slot, field, xs):
+        mixed = [
+            pltpu.roll(jnp.where(left, field[0, x + 1, ROWS, :], field[1, x + 1, ROWS, :]), 2 * x + 3, 1)
+            for x in xs
+        ]
+        z = zs[slot]
+        for x, m in zip(xs, mixed):
+            z = jnp.where((lane >> 1) == x + 1, m, z)
+        zs[slot] = z
+
+    def pack_last(slot, field, trip=4):
+        pack_planes(slot, field, list(range(N - trip, N)))
+
+    def pack_rows(slot, h, x, v, sides=(0, 1)):
         if 0 in sides:
-            ys[slot, 0, h, x] = low
+            ys[slot, 0, h, x] = v[0:1]
         if 1 in sides:
-            ys[slot, 1, h, x] = high
-
-    def put_low(z, a, x):
-        return jnp.where(lane == x + 1, pltpu.roll(a, x + 1, 1), z)
-
-    def put_high(z, b, x):
-        return jnp.where(lane == x + 1, pltpu.roll(b, x + 2, 1), z)
-
-    zero_plane = jnp.zeros((N, LANES), F32)
+            ys[slot, 1, h, x] = v[N - 1:N]
 
     def pack(slot, field, sides=(0, 1)):
-        def body(x, zz):
-            low, high = zz
-            for h in range(2):
-                for s in sides:
-                    row = 8 if s == 0 else 7 + N
-                    ys[slot, s, h, x] = field[h, x + 1, row:row + 1, :]
-            if 0 in sides:
-                low = put_low(low, field[0, x + 1, ROWS, :], x)
-            if 1 in sides:
-                high = put_high(high, field[1, x + 1, ROWS, :], x)
-            return low, high
-        low, high = lax.fori_loop(0, N, body, (zero_plane, zero_plane), unroll=2)
-        if 0 in sides:
-            zs[slot, 0] = low
-        if 1 in sides:
-            zs[slot, 1] = high
+        def body(xs, carry):
+            pack_planes(slot, field, xs)
+            for x in xs:
+                for h in range(2):
+                    for s in sides:
+                        row = 8 if s == 0 else 7 + N
+                        ys[slot, s, h, x] = field[h, x + 1, row:row + 1, :]
+            return carry
+        planes(body, 0, 8)
 
     def unpack_rows(slot, field, sides=(0, 1)):
         have = [flag((0, -1, 0)), flag((0, 1, 0))]
@@ -156,7 +167,10 @@
 
     def z_halo(slot, side):
         have = flag((0, 0, -1 if side == 0 else 1))
-        return jnp.where(have, zr[slot, side], zero_plane)
+        return jnp.where(have, pltpu.roll(zr[slot, side], 1 if side == 0 else LANES - 1, 1), zero_plane)
+
+    def z_halos(slot):
+        return jnp.where(odd, z_halo(slot, 0), z_halo(slot, 1))
 
     def edge_halo(slot, eslot, field, sign):
         side = 0 if sign > 0 else 1
@@ -167,7 +181,8 @@
         for h in range(2):
             got = exy[eslot, h]
             field[h, plane, row:row + 1, :] = jnp.where(have, got, jnp.zeros_like(got))
-        turn, at = (LANES - N, 0) if sign > 0 else (N, N + 1)
+        turn, at = (LANES // 2 + 1, 1) if sign > 0 else (2 * N - 1, 2 * N + 2)
+        whole = 1 if sign > 0 else LANES - 1
         beside = jnp.where(flag((step, 0, step)), exz[eslot], zero_plane)
         ze[eslot, ROWS, :] = jnp.where(lane == at, pltpu.roll(beside, turn, 1), z_halo(slot, side))
         tile_lane = lax.broadcasted_iota(jnp.int32, (8, LANES), 1)
@@ -175,7 +190,8 @@
         corner = jnp.where(flag((step, step, step)), exyz[eslot], zero_tile)
         across = jnp.where(flag((0, step, step)), eyz[eslot], zero_tile)
         tile = pl.ds(0, 8) if sign > 0 else pl.ds(8 + N, 8)
-        ze[eslot, tile, :] = jnp.where(tile_lane == at, pltpu.roll(corner, turn, 1), across)
+        ze[eslot, tile, :] = jnp.where(
+            tile_lane == at, pltpu.roll(corner, turn, 1), pltpu.roll(across, whole, 1))
 
     def clear_missing(field, planes=(0, PX - 1)):
         for plane in planes:
@@ -194,23 +210,32 @@
         ra, rb = pltpu.roll(a, LANES - 1, 1), pltpu.roll(b, LANES - 1, 1)
         return jnp.where(last_lane, rb, ra), jnp.where(last_lane, halo, rb)
 
-    def to_first(z, at):
-        return pltpu.roll(z, lax.rem(LANES - at, LANES), 1)
-
-    def to_last(z, at):
-        return pltpu.roll(z, LANES - 1 - at, 1)
-
-    def neighbours(field, x, low, high):
-        i = x + 1
-        a, b = field[0, i, ROWS, :], field[1, i, ROWS, :]
-        am, bm = z_below(a, b, to_first(low, i))
-        ap, bp = z_above(a, b, to_last(high, i))
+    def to_ends(z, i):
+        return pltpu.roll(z, LANES - 1 - 2 * i, 1)
+
+    def to_last(z, i):
+        return pltpu.roll(z, LANES - 1 - 2 * i, 1)
+
+    def to_first(z, i):
+        return pltpu.roll(z, LANES - 1 - 2 * i, 1)
+
+    def neighbours(field, xs, ends):
+        rolled = []
+        for x in xs:
+            a, b = field[0, x + 1, ROWS, :], field[1, x + 1, ROWS, :]
+            end = to_ends(ends, x + 1)
+            rolled.append((z_below(a, b, end), z_above(a, b, end)))
         out = []
-        for h, (m, p) in enumerate(((am, ap), (bm, bp))):
-            s = (field[h, i - 1, ROWS, :] + field[h, i + 1, ROWS, :]) + (
-                field[h, i, BELOW, :] + field[h, i, ABOVE, :])
-            out.append(s + (m + p))
-        return (a, b), out
+        for x, (m, p) in zip(xs, rolled):
+            i = x + 1
+            centre = [field[h, i, ROWS, :] for h in range(2)]
+            near = []
+            for h in range(2):
+                s = (field[h, i - 1, ROWS, :] + field[h, i + 1, ROWS, :]) + (
+                    field[h, i, BELOW, :] + field[h, i, ABOVE, :])
+                near.append(s + (m[h] + p[h]))
+            out.append((x, centre, near))
+        return out
 
     def fold(v):
         return (v[0:8] + v[8:16]) + (v[16:24] + v[24:32])
@@ -266,26 +291,21 @@
         for h in range(2):
             loads[name, h].wait()
 
-    def pressure_body(x, zz):
-        ph, rl, rh = zz
-        for h in range(2):
-            rho = cell[1, h, x + 1, ROWS, :]
-            p = 0.1 * rho * en[h, x]
-            cell[0, h, x + 1, ROWS, :] = p
-            ys[S_P, 1, h, x] = p[N - 1:N]
-            ys[S_RHO, 0, h, x] = rho[0:1]
-            ys[S_RHO, 1, h, x] = rho[N - 1:N]
-            if h == 0:
-                rl = put_low(rl, rho, x)
-            else:
-                ph = put_high(ph, p, x)
-                rh = put_high(rh, rho, x)
-        return ph, rl, rh
-
-    ph, rl, rh = lax.fori_loop(0, N, pressure_body, (zero_plane,) * 3)
-    zs[S_P, 1] = ph
-    zs[S_RHO, 0] = rl
-    zs[S_RHO, 1] = rh
+    def pressure_body(xs, carry):
+        back = lagging(xs)
+        pack_planes(S_P, cell.at[0], back)
+        pack_planes(S_RHO, cell.at[1], xs)
+        for x in xs:
+            for h in range(2):
+                rho = cell[1, h, x + 1, ROWS, :]
+                p = 0.1 * rho * en[h, x]
+                cell[0, h, x + 1, ROWS, :] = p
+                pack_rows(S_P, h, x, p, (1,))
+                pack_rows(S_RHO, h, x, rho)
+        return carry
+
+    planes(pressure_body)
+    pack_last(S_P, cell.at[0])
 
     pl.semaphore_wait(barrier, count + (nz - 1) + (nxy - 1))
     send_edges(S_P, E_P, 1)
@@ -298,20 +318,16 @@
             loads[name, h].wait()
 
     def advance(c):
-        def body(x, zz):
-            low, high = zz
-            for h in range(2):
-                v = w[c, h, x + 1, ROWS, :] + 0.6 * vel[c, h, x + 1, ROWS, :]
-                w[c, h, x + 1, ROWS, :] = v
-                pack_rows(S_W + c, h, x, v[0:1], v[N - 1:N])
-                if h == 0:
-                    low = put_low(low, v, x)
-                else:
-                    high = put_high(high, v, x)
-            return low, high
-        low, high = lax.fori_loop(0, N, body, (zero_plane,) * 2)
-        zs[S_W + c, 0] = low
-        zs[S_W + c, 1] = high
+        def body(xs, carry):
+            pack_planes(S_W + c, w.at[c], lagging(xs))
+            for x in xs:
+                for h in range(2):
+                    v = w[c, h, x + 1, ROWS, :] + 0.6 * vel[c, h, x + 1, ROWS, :]
+                    w[c, h, x + 1, ROWS, :] = v
+                    pack_rows(S_W + c, h, x, v)
+            return carry
+        planes(body)
+        pack_last(S_W + c, w.at[c])
         send_faces(S_W + c, w.at[c])
 
     for c in range(3):
@@ -345,14 +361,16 @@
         return tuple(
             t for h in range(2) for t in (ay[h] + aym[h], dy[h] + dym[h], aym[h] - ay[h]))
 
-    def force_body(x, before):
-        now = force_terms(x + 1)
-        for h in range(2):
-            r[0, h, x + 1, ROWS, :] = before[3 * h] - now[3 * h]
-            r[1, h, x + 1, ROWS, :] = before[3 * h + 1] + now[3 * h + 1]
-            r[2, h, x + 1, ROWS, :] = before[3 * h + 2] + now[3 * h + 2]
-        return now
-    lax.fori_loop(0, N, force_body, force_terms(0))
+    def force_body(i, before):
+        terms = [before] + [force_terms(4 * i + j + 1) for j in range(4)]
+        for j in range(4):
+            old, now = terms[j], terms[j + 1]
+            for h in range(2):
+                r[0, h, 4 * i + j + 1, ROWS, :] = old[3 * h] - now[3 * h]
+                r[1, h, 4 * i + j + 1, ROWS, :] = old[3 * h + 1] + now[3 * h + 1]
+                r[2, h, 4 * i + j + 1, ROWS, :] = old[3 * h + 2] + now[3 * h + 2]
+        return terms[4]
+    lax.fori_loop(0, N // 4, force_body, force_terms(0))
 
     for c in range(3):
         pack(S_R + c, r.at[c])
@@ -363,68 +381,64 @@
         aym = z_below(ay[0], ay[1], to_first(zrho, i))
         return ay[0] + aym[0], ay[1] + aym[1]
 
-    def mass_body(x, before):
-        now = mass_terms(x + 1)
-        for h in range(2):
-            mass[h, x] = 0.125 * (before[h] + now[h]) + 1.2
-        return now
-    lax.fori_loop(0, N, mass_body, mass_terms(0))
+    def mass_body(i, before):
+        terms = [before] + [mass_terms(4 * i + j + 1) for j in range(4)]
+        for j in range(4):
+            for h in range(2):
+                mass[h, 4 * i + j] = 0.125 * (terms[j][h] + terms[j + 1][h]) + 1.2
+        return terms[4]
+    lax.fori_loop(0, N // 4, mass_body, mass_terms(0))
 
     zero_tile = jnp.zeros((8, LANES), F32)
 
     def receive(slot, field):
         wait_faces(slot, field)
         unpack_rows(slot, field)
-        return z_halo(slot, 0), z_halo(slot, 1)
-
-    for c in range(3):
-        zl, zh = receive(S_R + c, r.at[c])
-
-        def image_body(x, carry, c=c, zl=zl, zh=zh):
-            low, high, m0, m1, m2 = carry
-            centre, near = neighbours(r.at[c], x, zl, zh)
-            for h in range(2):
-                image = mass[h, x] * centre[h] + 0.2 * near[h]
-                q[c, h, x + 1, ROWS, :] = image
-                nr[c, h, x] = near[h]
-                m0 = m0 + fold(centre[h] * centre[h])
-                m1 = m1 + fold(centre[h] * image)
-                m2 = m2 + fold(image * image)
-                pack_rows(S_Q + c, h, x, image[0:1], image[N - 1:N])
-                if h == 0:
-                    low = put_low(low, image, x)
-                else:
-                    high = put_high(high, image, x)
-            return low, high, m0, m1, m2
-        low, high, m0, m1, m2 = lax.fori_loop(
-            0, N, image_body, (zero_plane, zero_plane, zero_tile, zero_tile, zero_tile))
-        zs[S_Q + c, 0] = low
-        zs[S_Q + c, 1] = high
+        return z_halos(slot)
+
+    for c in range(3):
+        ends = receive(S_R + c, r.at[c])
+
+        def image_body(xs, carry, c=c, ends=ends):
+            m0, m1, m2 = carry
+            pack_planes(S_Q + c, q.at[c], lagging(xs))
+            for x, centre, near in neighbours(r.at[c], xs, ends):
+                for h in range(2):
+                    image = mass[h, x] * centre[h] + 0.2 * near[h]
+                    q[c, h, x + 1, ROWS, :] = image
+                    nr[c, h, x] = near[h]
+                    m0 = m0 + fold(centre[h] * centre[h])
+                    m1 = m1 + fold(centre[h] * image)
+                    m2 = m2 + fold(image * image)
+                    pack_rows(S_Q + c, h, x, image)
+            return m0, m1, m2
+        moments = planes(image_body, (zero_tile, zero_tile, zero_tile))
+        pack_last(S_Q + c, q.at[c])
         send_faces(S_Q + c, q.at[c])
-        for k, m in enumerate((m0, m1, m2)):
+        for k, m in enumerate(moments):
             mom[4 * c + k:4 * c + k + 1, :] = jnp.sum(m, axis=0, keepdims=True)
 
     def near_w(c):
-        zl, zh = receive(S_W + c, w.at[c])
-
-        def body(x, _):
-            _c, near = neighbours(w.at[c], x, zl, zh)
-            for h in range(2):
-                nw[c, h, x] = near[h]
-            return 0
-        lax.fori_loop(0, N, body, 0)
+        ends = receive(S_W + c, w.at[c])
+
+        def body(xs, carry):
+            for x, _centre, near in neighbours(w.at[c], xs, ends):
+                for h in range(2):
+                    nw[c, h, x] = near[h]
+            return carry
+        planes(body)
 
     near_w(0)
     for c in range(3):
-        zl, zh = receive(S_Q + c, q.at[c])
-
-        def second_body(x, m3, c=c, zl=zl, zh=zh):
-            centre, near = neighbours(q.at[c], x, zl, zh)
-            for h in range(2):
-                nq[c, h, x] = near[h]
-                m3 = m3 + fold(centre[h] * (mass[h, x] * centre[h] + 0.2 * near[h]))
+        ends = receive(S_Q + c, q.at[c])
+
+        def second_body(xs, m3, c=c, ends=ends):
+            for x, centre, near in neighbours(q.at[c], xs, ends):
+                for h in range(2):
+                    nq[c, h, x] = near[h]
+                    m3 = m3 + fold(centre[h] * (mass[h, x] * centre[h] + 0.2 * near[h]))
             return m3
-        m3 = lax.fori_loop(0, N, second_body, zero_tile)
+        m3 = planes(second_body, zero_tile)
         mom[4 * c + 3:4 * c + 4, :] = jnp.sum(m3, axis=0, keepdims=True)
     mom[12:16, :] = jnp.zeros((4, LANES), F32)
 
@@ -480,29 +494,25 @@
         c1 = jnp.broadcast_to(a1 + a2 * b1, (N, LANES))
         c2 = jnp.broadcast_to(-a1 * a2, (N, LANES))
 
-        def step_body(x, carry, c=c, c1=c1, c2=c2):
-            low, high = carry
-            i = x + 1
-            for h in range(2):
-                a = c1 * r[c, h, i, ROWS, :] + c2 * q[c, h, i, ROWS, :]
-                acc[c, h, x] = a
-                v = vel[c, h, i, ROWS, :] + 0.6 * a
-                vel[c, h, i, ROWS, :] = v
-                moved = w[c, h, i, ROWS, :] + 0.36 * a
-                w[c, h, i, ROWS, :] = moved
-                near = nw[c, h, x] + 0.36 * (c1 * nr[c, h, x] + c2 * nq[c, h, x])
-                u = moved + free[h, x] * (near * (1.0 / 6.0) - moved)
-                one[c, h, i, ROWS, :] = u
-                pack_rows(S_ONE + c, h, x, u[0:1], u[N - 1:N])
-                if h == 0:
-                    low = put_low(low, u, x)
-                else:
-                    high = put_high(high, u, x)
-            return low, high
+        def step_body(xs, carry, c=c, c1=c1, c2=c2):
+            pack_planes(S_ONE + c, one.at[c], lagging(xs))
+            for x in xs:
+                i = x + 1
+                for h in range(2):
+                    a = c1 * r[c, h, i, ROWS, :] + c2 * q[c, h, i, ROWS, :]
+                    acc[c, h, x] = a
+                    v = vel[c, h, i, ROWS, :] + 0.6 * a
+                    vel[c, h, i, ROWS, :] = v
+                    moved = w[c, h, i, ROWS, :] + 0.36 * a
+                    w[c, h, i, ROWS, :] = moved
+                    near = nw[c, h, x] + 0.36 * (c1 * nr[c, h, x] + c2 * nq[c, h, x])
+                    u = moved + free[h, x] * (near * (1.0 / 6.0) - moved)
+                    one[c, h, i, ROWS, :] = u
+                    pack_rows(S_ONE + c, h, x, u)
+            return carry
         drain(S_W + c)
-        low, high = lax.fori_loop(0, N, step_body, (zero_plane,) * 2)
-        zs[S_ONE + c, 0] = low
-        zs[S_ONE + c, 1] = high
+        planes(step_body)
+        pack_last(S_ONE + c, one.at[c])
         send_faces(S_ONE + c, one.at[c])
     for c in range(3):
         pack(S_VEL + c, vel.at[c], (0,))
@@ -512,23 +522,24 @@
             write(acc.at[c, h], a_out.at[c, :, :, halves(h)], c, h)
             write(vel.at[c, h, pl.ds(1, N), ROWS, :], v_out.at[c, :, :, halves(h)], 3 + c, h)
 
-    def swept(field, c, x, zl, zh):
-        centre, near = neighbours(field.at[c], x, zl, zh)
-        return [centre[h] + free[h, x] * (near[h] * (1.0 / 6.0) - centre[h]) for h in range(2)]
-
-    for c in range(3):
-        zl, zh = receive(S_ONE + c, one.at[c])
-
-        def sweep_body(x, carry, c=c, zl=zl, zh=zh):
-            low, high = carry
-            u = swept(one, c, x, zl, zh)
-            for h in range(2):
-                two[c, h, x + 1, ROWS, :] = u[h]
-                pack_rows(S_TWO + c, h, x, u[h][0:1], u[h][N - 1:N])
-            return put_low(low, u[0], x), put_high(high, u[1], x)
-        low, high = lax.fori_loop(0, N, sweep_body, (zero_plane,) * 2)
-        zs[S_TWO + c, 0] = low
-        zs[S_TWO + c, 1] = high
+    def swept(field, c, xs, ends):
+        return [
+            (x, [centre[h] + free[h, x] * (near[h] * (1.0 / 6.0) - centre[h]) for h in range(2)])
+            for x, centre, near in neighbours(field.at[c], xs, ends)
+        ]
+
+    for c in range(3):
+        ends = receive(S_ONE + c, one.at[c])
+
+        def sweep_body(xs, carry, c=c, ends=ends):
+            pack_planes(S_TWO + c, two.at[c], lagging(xs))
+            for x, u in swept(one, c, xs, ends):
+                for h in range(2):
+                    two[c, h, x + 1, ROWS, :] = u[h]
+                    pack_rows(S_TWO + c, h, x, u[h])
+            return carry
+        planes(sweep_body)
+        pack_last(S_TWO + c, two.at[c])
         send_faces(S_TWO + c, two.at[c])
 
     for c in range(3):
@@ -561,40 +572,38 @@
             minus.append(flat - along_x)
         return plus, minus
 
-    def div_body(x, carry):
-        b0, b1, low, high = carry
-        plus, minus = div_terms(x + 2)
-        for h, before in enumerate((b0, b1)):
-            spread = before + plus[h]
-            value = cell[1, h, x + 1, ROWS, :] * (en[h, x] * (1.0 - 0.06 * spread))
-            de[h, x + 1, ROWS, :] = value
-            pack_rows(S_DE, h, x, value[0:1], value[N - 1:N])
-            if h == 0:
-                low = put_low(low, value, x)
-            else:
-                high = put_high(high, value, x)
-        return minus[0], minus[1], low, high
-    _plus, minus = div_terms(1)
-    _0, _1, low, high = lax.fori_loop(0, N, div_body, (minus[0], minus[1], zero_plane, zero_plane))
-    zs[S_DE, 0] = low
-    zs[S_DE, 1] = high
+    def div_body(k, before):
+        back = jnp.maximum(2 * k - 2, 0)
+        pack_planes(S_DE, de, [back, back + 1])
+        for j in range(2):
+            x = 2 * k + j
+            plus, minus = div_terms(x + 2)
+            for h in range(2):
+                spread = before[h] + plus[h]
+                value = cell[1, h, x + 1, ROWS, :] * (en[h, x] * (1.0 - 0.06 * spread))
+                de[h, x + 1, ROWS, :] = value
+                pack_rows(S_DE, h, x, value)
+            before = minus
+        return tuple(before)
+    lax.fori_loop(0, N // 2, div_body, tuple(div_terms(1)[1]))
+    pack_last(S_DE, de, 2)
     send_faces(S_DE, de)
 
     for c in range(3):
-        zl, zh = receive(S_TWO + c, two.at[c])
-
-        def last_body(x, low, c=c, zl=zl, zh=zh):
-            u = swept(two, c, x, zl, zh)
-            for h in range(2):
-                nw[c, h, x] = u[h]
-                s = u[h] - w[c, h, x + 1, ROWS, :]
-                sh[c, h, x + 1, ROWS, :] = s
-                pack_rows(S_SH + c, h, x, s[0:1], None, (0,))
-                if h == 0:
-                    low = put_low(low, s, x)
-            return low
+        ends = receive(S_TWO + c, two.at[c])
         drain(S_Q + c)
-        zs[S_SH + c, 0] = lax.fori_loop(0, N, last_body, zero_plane)
+
+        def last_body(xs, carry, c=c, ends=ends):
+            pack_planes(S_SH + c, sh.at[c], lagging(xs))
+            for x, u in swept(two, c, xs, ends):
+                for h in range(2):
+                    nw[c, h, x] = u[h]
+                    s = u[h] - w[c, h, x + 1, ROWS, :]
+                    sh[c, h, x + 1, ROWS, :] = s
+                    pack_rows(S_SH + c, h, x, s, (0,))
+            return carry
+        planes(last_body)
+        pack_last(S_SH + c, sh.at[c])
         send_faces(S_SH + c, sh.at[c], (4, 2, 0))
         send_edges(S_SH + c, E_SH + c, -1)
         for h in range(2):
@@ -611,11 +620,13 @@
     z_ax = zx[0] + zx[1]
     wide = pl.ds(8, 40)
     z_y = ze[E_SH + 1, wide, :]
-    z_y = z_y + pltpu.roll(z_y, LANES - 1, 1)
+    z_y = z_y + pltpu.roll(z_y, LANES - 2, 1)
     z_z = zz3[0] + zz3[1]
-    z_z = 0.25 * (z_z + pltpu.roll(z_z, LANES - 1, 1))
-    low_q = [z_halo(slot, 0) for slot in slots]
-    top_g = [z_z * jnp.where(z_z > 0, z_halo(slot, 1), zs[slot, 1]) for slot in slots]
+    z_z = 0.25 * (z_z + pltpu.roll(z_z, LANES - 2, 1))
+    ends_q = [
+        jnp.where(odd, z_halo(slot, 0), z_z * jnp.where(z_z > 0, z_halo(slot, 1), zs[slot]))
+        for slot in slots
+    ]
     wide_last = lax.broadcasted_iota(jnp.int32, (40, LANES), 1) == LANES - 1
 
     def flux_x(i):
@@ -628,32 +639,52 @@
                 out.append(s * jnp.where(s > 0, field[h, i, ROWS, :], field[h, i - 1, ROWS, :]))
         return tuple(out)
 
-    def remap_body(x, before):
-        i = x + 1
-        now = flux_x(i + 1)
-        t = [sh[1, h, i, wide, :] + sh[1, h, i + 1, wide, :] for h in range(2)]
-        ra, rb = [pltpu.roll(v, LANES - 1, 1) for v in t]
-        up = (jnp.where(wide_last, rb, ra), jnp.where(wide_last, to_last(z_y, i), rb))
-        for h in range(2):
-            s = 0.25 * (t[h] + up[h])
+    def remap_x(k, before):
+        for j in range(2):
+            x = 2 * k + j
+            now = flux_x(x + 2)
+            for h in range(2):
+                for f, field in enumerate(fields):
+                    nr[f, h, x] = field[h, x + 1, ROWS, :] + (now[2 * h + f] - before[2 * h + f])
+            before = now
+        return before
+    lax.fori_loop(0, N // 2, remap_x, flux_x(1))
+
+    def remap_y(xs, carry):
+        for j, x in enumerate(xs):
+            i = x + 1
+            t = [sh[1, h, i, wide, :] + sh[1, h, i + 1, wide, :] for h in range(2)]
+            ra, rb = [pltpu.roll(v, LANES - 1, 1) for v in t]
+            up = (jnp.where(wide_last, rb, ra), jnp.where(wide_last, to_last(z_y, i), rb))
+            for h in range(2):
+                s = 0.25 * (t[h] + up[h])
+                for f, field in enumerate(fields):
+                    gy[j, f, h] = s * jnp.where(s > 0, field[h, i, wide, :], field[h, i, pl.ds(7, 40), :])
+        for j, x in enumerate(xs):
+            for h in range(2):
+                for f in range(2):
+                    nr[f, h, x] = nr[f, h, x] + (gy[j, f, h, 1:N + 1, :] - gy[j, f, h, 0:N, :])
+        return carry
+    planes(remap_y, 0, 2)
+
+    def remap_z(xs, carry):
+        for x in xs:
+            i = x + 1
+            s = [
+                0.25 * ((sh[2, h, i, ROWS, :] + sh[2, h, i, ABOVE, :])
+                        + (sh[2, h, i + 1, ROWS, :] + sh[2, h, i + 1, ABOVE, :]))
+                for h in range(2)
+            ]
             for f, field in enumerate(fields):
-                gy[f, h] = s * jnp.where(s > 0, field[h, i, wide, :], field[h, i, pl.ds(7, 40), :])
-        s = [
-            0.25 * ((sh[2, h, i, ROWS, :] + sh[2, h, i, ABOVE, :])
-                    + (sh[2, h, i + 1, ROWS, :] + sh[2, h, i + 1, ABOVE, :]))
-            for h in range(2)
-        ]
-        for f, field in enumerate(fields):
-            own = [field[h, i, ROWS, :] for h in range(2)]
-            under = z_below(own[0], own[1], to_first(low_q[f], i))
-            g = [s[h] * jnp.where(s[h] > 0, own[h], under[h]) for h in range(2)]
-            over = z_above(g[0], g[1], to_last(top_g[f], i))
-            for h in range(2):
-                nr[f, h, x] = (
-                    own[h] + (now[2 * h + f] - before[2 * h + f])
-                    + (gy[f, h, 1:N + 1, :] - gy[f, h, 0:N, :]) + (over[h] - g[h]))
-        return now
-    lax.fori_loop(0, N, remap_body, flux_x(1))
+                own = [field[h, i, ROWS, :] for h in range(2)]
+                end = to_ends(ends_q[f], i)
+                under = z_below(own[0], own[1], end)
+                g = [s[h] * jnp.where(s[h] > 0, own[h], under[h]) for h in range(2)]
+                over = z_above(g[0], g[1], end)
+                for h in range(2):
+                    nr[f, h, x] = nr[f, h, x] + (over[h] - g[h])
+        return carry
+    planes(remap_z, 0, 2)
     for f, out in enumerate((d_out, e_out)):
         for h in range(2):
             write(nr.at[f, h], out.at[:, :, halves(h)], 9 + f, h)
@@ -698,14 +729,14 @@
                 padded(3), padded(3), padded(),
                 pltpu.VMEM((SLOTS, 2, 2, N, 1, LANES), F32),
                 pltpu.VMEM((SLOTS, 2, 2, N, 1, LANES), F32),
-                pltpu.VMEM((SLOTS, 2, N, LANES), F32),
+                pltpu.VMEM((SLOTS, N, LANES), F32),
                 pltpu.VMEM((SLOTS, 2, N, LANES), F32),
                 pltpu.VMEM((EDGES, 2, 1, LANES), F32),
                 pltpu.VMEM((EDGES, N, LANES), F32),
                 pltpu.VMEM((EDGES, 8, LANES), F32),
                 pltpu.VMEM((EDGES, 8, LANES), F32),
                 pltpu.VMEM((EDGES, PY, LANES), F32),
-                pltpu.VMEM((2, 2, 40, LANES), F32),
+                pltpu.VMEM((2, 2, 2, 40, LANES), F32),
                 pltpu.VMEM((16, LANES), F32),
                 pltpu.VMEM((sizes[2], 1, LANES), F32),
                 pltpu.VMEM((sizes[0] * sizes[1], 1, LANES), F32),

time: 146 us -> 83.9 us (0.57)
  Pallas kernels: 134 us -> 72 us
    pallas_call x1, Pallas kernels: 134 us -> 72 us  [on_device(): pl.pallas_call(body, name='lagrangian_step', out_shape=(v3, v3, v3, v1, v...]
where the time goes in v2:
time: 83.9 us; the launch traced here: 83.7 us
  Pallas kernels  72 us (86%)
  local copies, waits for them, and re-layouts  11 us (13%)
    pallas_call x1, Pallas kernels, on_device(): pl.pallas_call(body, name='lagrangian_step', out_shape=(v3, v3, v3, v1, v...  72 us
    unnamed x13, local copies, waits for them, and re-layouts  11 us

profile of v2, /device:TPU:1, one launch (start us, length us, event | category | flops | bytes accessed | tf_op | source)
XLA Modules:
  0.0 83.7 jit_solution(13916685479486073301)
XLA Ops:
  0.6 72.0 %lagrangian_step.1 = (f32[3,32,32,256]{3,2,1,0:T(8,128)}, f32[3,32,32,256]{3,2,1,0:T(8,128)}, f32[3,32,32,256]{3,2,1,0:T(8,128)}, f32[32,32,256]{2,1,0:T(8,128)}, f32[32,32,256]{2,1,0:T(8,128)}) custom-call(f32[3,32,32,256]{3,2,1,0:T(8,128)} %refs_0_.1, f32[3,32,32,256]{3,2,1,0:T(8,128)} %refs_1_.1, f32[32,32,256]{2,1,0:T(8,128)} %refs_2_.1, ...), custom_call_target="tpu_custom_call" | custom-call | tf_op jit(solution)/shard_map/lagrangian_step/pallas_call | solution.py:720
  72.6 0.0 copy-start.1
  72.7 4.1 %copy.15 = f32[3,32,32,256]{3,2,1,0:T(8,128)} copy(f32[3,32,32,256]{3,2,1,0:T(8,128)} %get-tuple-element.10) | data formatting | bytes 6291456
  76.8 0.0 copy-done.1
  76.8 0.0 copy-start
  76.8 1.7 %copy.16 = f32[3,32,32,256]{3,2,1,0:T(8,128)} copy(f32[3,32,32,256]{3,2,1,0:T(8,128)S(1)} %copy-done.1) | data formatting | bytes 6291456
  78.4 1.4 %copy-done = f32[3,32,32,256]{3,2,1,0:T(8,128)S(1)} copy-done((f32[3,32,32,256]{3,2,1,0:T(8,128)S(1)}, f32[3,32,32,256]{3,2,1,0:T(8,128)}, u32[]{:S(2)}) %copy-start) | copy-done | bytes 3145752
  79.8 0.0 copy-start.3
  79.8 0.0 copy-start.2
  79.8 1.7 %copy.17 = f32[3,32,32,256]{3,2,1,0:T(8,128)} copy(f32[3,32,32,256]{3,2,1,0:T(8,128)S(1)} %copy-done) | data formatting | bytes 6291456
  81.5 0.3 copy-done.3
  81.8 1.0 %copy.18 = f32[32,32,256]{2,1,0:T(8,128)} copy(f32[32,32,256]{2,1,0:T(8,128)S(1)} %copy-done.3) | data formatting | bytes 2097152
  82.7 0.0 copy-done.2
  82.7 1.0 %copy.19 = f32[32,32,256]{2,1,0:T(8,128)} copy(f32[32,32,256]{2,1,0:T(8,128)S(1)} %copy-done.2) | data formatting | bytes 2097152
Async XLA Ops:
  72.6 4.1 %copy-start.1 = (f32[3,32,32,256]{3,2,1,0:T(8,128)S(1)}, f32[3,32,32,256]{3,2,1,0:T(8,128)}, u32[]{:S(2)}) copy-start(f32[3,32,32,256]{3,2,1,0:T(8,128)} %get-tuple-element.11) | copy-start | bytes 9437188
  76.8 3.0 %copy-start = (f32[3,32,32,256]{3,2,1,0:T(8,128)S(1)}, f32[3,32,32,256]{3,2,1,0:T(8,128)}, u32[]{:S(2)}) copy-start(f32[3,32,32,256]{3,2,1,0:T(8,128)} %get-tuple-element.12) | copy-start | bytes 9437188
  79.8 2.0 %copy-start.3 = (f32[32,32,256]{2,1,0:T(8,128)S(1)}, f32[32,32,256]{2,1,0:T(8,128)}, u32[]{:S(2)}) copy-start(f32[32,32,256]{2,1,0:T(8,128)} %get-tuple-element.13) | copy-start | bytes 3145732
  79.8 2.9 %copy-start.2 = (f32[32,32,256]{2,1,0:T(8,128)S(1)}, f32[32,32,256]{2,1,0:T(8,128)}, u32[]{:S(2)}) copy-start(f32[32,32,256]{2,1,0:T(8,128)} %get-tuple-element.14) | copy-start | bytes 3145732

commit v3 on v2

--- a/solution.py
+++ b/solution.py
@@ -21,17 +21,48 @@
 EDGES = 8
 
 
+def _lane():
+    return lax.broadcasted_iota(jnp.int32, (N, LANES), 1)
+
+
+def planes(body, init=0, trip=4, start=0, stop=N):
+    def run(i, carry):
+        return body([i * trip + j for j in range(trip)], carry)
+    return lax.fori_loop(start // trip, stop // trip, run, init)
+
+
+def z_below(a, b, halo):
+    ra, rb = pltpu.roll(a, 1, 1), pltpu.roll(b, 1, 1)
+    return jnp.where(_lane() == 0, halo, ra), jnp.where(_lane() == 0, ra, rb)
+
+
+def z_above(a, b, halo):
+    ra, rb = pltpu.roll(a, LANES - 1, 1), pltpu.roll(b, LANES - 1, 1)
+    return jnp.where(_lane() == LANES - 1, rb, ra), jnp.where(_lane() == LANES - 1, halo, rb)
+
+
+def to_ends(z, i):
+    return pltpu.roll(z, LANES - 1 - 2 * i, 1)
+
+
+def to_last(z, i):
+    return pltpu.roll(z, LANES - 1 - 2 * i, 1)
+
+
+def to_first(z, i):
+    return pltpu.roll(z, LANES - 1 - 2 * i, 1)
+
+
 def kernel(
     sizes,
     pos_in, vel_in, rho_in, en_in, pin_in,
-    v_out, a_out, r_out, d_out, e_out,
-    cell, en, vel, w, r, q, nw, nr, nq, pin, free, mass, acc, one, two, de,
-    ys, yr, zs, zr, exy, exz, eyz, exyz, ze, gy, mom, ar1, ar2,
-    in_sem, out_sem, face_s, face_r, edge_s, edge_r, a1s, a1r, a2s, a2r,
+    vel, acc, relaxed, sh, de, rho_f, tab,
+    pres, en, w, r, q, nw, nr, nq, pin, free, mass, one, two,
+    ys, yr, zs, zr, exy, exz, eyz, exyz, ze, mom, ar1, ar2,
+    in_sem, face_s, face_r, edge_s, edge_r, a1s, a1r, a2s, a2r,
 ):
     names = ("bx", "by", "bz")
     here = [lax.axis_index(name) for name in names]
-    sh = q
 
     def exists(step):
         ok = None
@@ -53,8 +84,6 @@
 
     steps = ((-1, 0, 0), (1, 0, 0), (0, -1, 0), (0, 1, 0), (0, 0, -1), (0, 0, 1))
     lane = lax.broadcasted_iota(jnp.int32, (N, LANES), 1)
-    first_lane = lane == 0
-    last_lane = lane == LANES - 1
 
     def face_copy(slot, field, d):
         if d < 2:
@@ -114,11 +143,6 @@
     odd = lane % 2 == 1
     left = lane < LANES // 2
 
-    def planes(body, init=0, trip=4):
-        def run(i, carry):
-            return body([i * trip + j for j in range(trip)], carry)
-        return lax.fori_loop(0, N // trip, run, init)
-
     def lagging(xs):
         back = jnp.minimum(xs[0], len(xs))
         return [x - back for x in xs]
@@ -202,23 +226,6 @@
                 for h in range(2):
                     field[h, plane, ROWS, :] = zero_plane
 
-    def z_below(a, b, halo):
-        ra, rb = pltpu.roll(a, 1, 1), pltpu.roll(b, 1, 1)
-        return jnp.where(first_lane, halo, ra), jnp.where(first_lane, ra, rb)
-
-    def z_above(a, b, halo):
-        ra, rb = pltpu.roll(a, LANES - 1, 1), pltpu.roll(b, LANES - 1, 1)
-        return jnp.where(last_lane, rb, ra), jnp.where(last_lane, halo, rb)
-
-    def to_ends(z, i):
-        return pltpu.roll(z, LANES - 1 - 2 * i, 1)
-
-    def to_last(z, i):
-        return pltpu.roll(z, LANES - 1 - 2 * i, 1)
-
-    def to_first(z, i):
-        return pltpu.roll(z, LANES - 1 - 2 * i, 1)
-
     def neighbours(field, xs, ends):
         rolled = []
         for x in xs:
@@ -246,7 +253,7 @@
     loads = {}
     for h in range(2):
         loads["rho", h] = pltpu.make_async_copy(
-            rho_in.at[:, :, halves(h)], cell.at[1, h, pl.ds(1, N), ROWS, :], in_sem.at[0, h])
+            rho_in.at[:, :, halves(h)], rho_f.at[h, pl.ds(1, N), ROWS, :], in_sem.at[0, h])
         loads["en", h] = pltpu.make_async_copy(en_in.at[:, :, halves(h)], en.at[h], in_sem.at[1, h])
         loads["vel", h] = pltpu.make_async_copy(
             vel_in.at[:, :, :, halves(h)], vel.at[:, h, pl.ds(1, N), ROWS, :], in_sem.at[2, h])
@@ -257,13 +264,14 @@
         for h in range(2):
             loads[name, h].start()
 
-    clear_missing(cell.at[0], (0,))
-    clear_missing(cell.at[1])
+    clear_missing(pres, (0,))
+    clear_missing(rho_f)
     clear_missing(de)
     for c in range(3):
         for field in (w, r, q, one, two):
             clear_missing(field.at[c])
-        clear_missing(vel.at[c], (PX - 1,))
+        for field in (vel, sh):
+            clear_missing(field.at[c], (PX - 1,))
 
     barrier = pltpu.get_barrier_semaphore()
     around = [s for s in ((i, j, k) for i in (0, 1) for j in (0, 1) for k in (0, 1)) if any(s)]
@@ -293,25 +301,25 @@
 
     def pressure_body(xs, carry):
         back = lagging(xs)
-        pack_planes(S_P, cell.at[0], back)
-        pack_planes(S_RHO, cell.at[1], xs)
+        pack_planes(S_P, pres, back)
+        pack_planes(S_RHO, rho_f, xs)
         for x in xs:
             for h in range(2):
-                rho = cell[1, h, x + 1, ROWS, :]
+                rho = rho_f[h, x + 1, ROWS, :]
                 p = 0.1 * rho * en[h, x]
-                cell[0, h, x + 1, ROWS, :] = p
+                pres[h, x + 1, ROWS, :] = p
                 pack_rows(S_P, h, x, p, (1,))
                 pack_rows(S_RHO, h, x, rho)
         return carry
 
     planes(pressure_body)
-    pack_last(S_P, cell.at[0])
+    pack_last(S_P, pres)
 
     pl.semaphore_wait(barrier, count + (nz - 1) + (nxy - 1))
     send_edges(S_P, E_P, 1)
     send_edges(S_RHO, E_RHO, 1)
-    send_faces(S_P, cell.at[0], (5, 3, 1))
-    send_faces(S_RHO, cell.at[1], (5, 3, 1, 4, 2, 0))
+    send_faces(S_P, pres, (5, 3, 1))
+    send_faces(S_RHO, rho_f, (5, 3, 1, 4, 2, 0))
 
     for name in ("vel", "pos", "pin"):
         for h in range(2):
@@ -339,13 +347,13 @@
         return 0
     lax.fori_loop(0, N, mask_body, 0)
 
-    wait_faces(S_P, cell.at[0], (5, 3, 1))
+    wait_faces(S_P, pres, (5, 3, 1))
     wait_edges(S_P, E_P, 1)
-    wait_faces(S_RHO, cell.at[1])
+    wait_faces(S_RHO, rho_f)
     wait_edges(S_RHO, E_RHO, 1)
-    edge_halo(S_P, E_P, cell.at[0], 1)
-    edge_halo(S_RHO, E_RHO, cell.at[1], 1)
-    unpack_rows(S_RHO, cell.at[1], (1,))
+    edge_halo(S_P, E_P, pres, 1)
+    edge_halo(S_RHO, E_RHO, rho_f, 1)
+    unpack_rows(S_RHO, rho_f, (1,))
     zay = ze[E_P, ROWS, :] + ze[E_P, BELOW, :]
     zdy = ze[E_P, BELOW, :] - ze[E_P, ROWS, :]
     zrho = ze[E_RHO, ROWS, :] + ze[E_RHO, BELOW, :]
@@ -353,7 +361,7 @@
     def force_terms(i):
         ay, dy = [], []
         for h in range(2):
-            c, b = cell[0, h, i, ROWS, :], cell[0, h, i, BELOW, :]
+            c, b = pres[h, i, ROWS, :], pres[h, i, BELOW, :]
             ay.append(c + b)
             dy.append(b - c)
         aym = z_below(ay[0], ay[1], to_first(zay, i))
@@ -377,7 +385,7 @@
         send_faces(S_R + c, r.at[c])
 
     def mass_terms(i):
-        ay = [cell[1, h, i, ROWS, :] + cell[1, h, i, BELOW, :] for h in range(2)]
+        ay = [rho_f[h, i, ROWS, :] + rho_f[h, i, BELOW, :] for h in range(2)]
         aym = z_below(ay[0], ay[1], to_first(zrho, i))
         return ay[0] + aym[0], ay[1] + aym[1]
 
@@ -477,13 +485,6 @@
 
     def pick(k):
         return jnp.sum(jnp.where(row_lane == k, sums, 0.0), axis=1, keepdims=True)
-
-    outs = []
-
-    def write(src, dst, i, h):
-        copy = pltpu.make_async_copy(src, dst, out_sem.at[i, h])
-        copy.start()
-        outs.append(copy)
 
     for c in range(3):
         m0, m1, m2, m3 = [pick(4 * c + k) for k in range(4)]
@@ -518,9 +519,6 @@
         pack(S_VEL + c, vel.at[c], (0,))
         send_faces(S_VEL + c, vel.at[c], (0, 2, 4))
         send_edges(S_VEL + c, E_VEL + c, -1)
-        for h in range(2):
-            write(acc.at[c, h], a_out.at[c, :, :, halves(h)], c, h)
-            write(vel.at[c, h, pl.ds(1, N), ROWS, :], v_out.at[c, :, :, halves(h)], 3 + c, h)
 
     def swept(field, c, xs, ends):
         return [
@@ -580,7 +578,7 @@
             plus, minus = div_terms(x + 2)
             for h in range(2):
                 spread = before[h] + plus[h]
-                value = cell[1, h, x + 1, ROWS, :] * (en[h, x] * (1.0 - 0.06 * spread))
+                value = rho_f[h, x + 1, ROWS, :] * (en[h, x] * (1.0 - 0.06 * spread))
                 de[h, x + 1, ROWS, :] = value
                 pack_rows(S_DE, h, x, value)
             before = minus
@@ -591,13 +589,12 @@
 
     for c in range(3):
         ends = receive(S_TWO + c, two.at[c])
-        drain(S_Q + c)
 
         def last_body(xs, carry, c=c, ends=ends):
             pack_planes(S_SH + c, sh.at[c], lagging(xs))
             for x, u in swept(two, c, xs, ends):
                 for h in range(2):
-                    nw[c, h, x] = u[h]
+                    relaxed[c, h, x] = u[h]
                     s = u[h] - w[c, h, x + 1, ROWS, :]
                     sh[c, h, x + 1, ROWS, :] = s
                     pack_rows(S_SH + c, h, x, s, (0,))
@@ -606,32 +603,55 @@
         pack_last(S_SH + c, sh.at[c])
         send_faces(S_SH + c, sh.at[c], (4, 2, 0))
         send_edges(S_SH + c, E_SH + c, -1)
-        for h in range(2):
-            write(nw.at[c, h], r_out.at[c, :, :, halves(h)], 6 + c, h)
-
-    fields = (cell.at[1], de)
-    slots = (S_RHO, S_DE)
+
     receive(S_DE, de)
     for c in range(3):
         wait_faces(S_SH + c, sh.at[c], (4, 2, 0))
         wait_edges(S_SH + c, E_SH + c, -1)
         edge_halo(S_SH + c, E_SH + c, sh.at[c], -1)
     zx, zz3 = rows_up(E_SH), rows_up(E_SH + 2)
-    z_ax = zx[0] + zx[1]
-    wide = pl.ds(8, 40)
-    z_y = ze[E_SH + 1, wide, :]
-    z_y = z_y + pltpu.roll(z_y, LANES - 2, 1)
+    tab[0, 0:N, :] = zx[0] + zx[1]
+    z_y = ze[E_SH + 1, pl.ds(8, 40), :]
+    tab[1] = z_y + pltpu.roll(z_y, LANES - 2, 1)
     z_z = zz3[0] + zz3[1]
     z_z = 0.25 * (z_z + pltpu.roll(z_z, LANES - 2, 1))
-    ends_q = [
-        jnp.where(odd, z_halo(slot, 0), z_z * jnp.where(z_z > 0, z_halo(slot, 1), zs[slot]))
-        for slot in slots
-    ]
+    for f, slot in enumerate((S_RHO, S_DE)):
+        tab[2 + f, 0:N, :] = jnp.where(
+            odd, z_halo(slot, 0), z_z * jnp.where(z_z > 0, z_halo(slot, 1), zs[slot]))
+
+    for slot in tuple(sent):
+        drain(slot)
+    for copy in along + across:
+        copy.wait_send()
+
+
+def remap(
+    vel, acc, relaxed, sh, de, rho_f, tab,
+    v_out, a_out, r_out, d_out, e_out,
+    nr, gy, out_sem,
+):
+    fields = (rho_f, de)
+    wide = pl.ds(8, 40)
+    outs = []
+
+    def halves(k):
+        return pl.ds(k * LANES, LANES)
+
+    def write(src, dst, i, h):
+        copy = pltpu.make_async_copy(src, dst, out_sem.at[i, h])
+        copy.start()
+        outs.append(copy)
+
+    for c in range(3):
+        for h in range(2):
+            write(acc.at[c, h], a_out.at[c, :, :, halves(h)], c, h)
+            write(vel.at[c, h, pl.ds(1, N), ROWS, :], v_out.at[c, :, :, halves(h)], 3 + c, h)
+            write(relaxed.at[c, h], r_out.at[c, :, :, halves(h)], 6 + c, h)
     wide_last = lax.broadcasted_iota(jnp.int32, (40, LANES), 1) == LANES - 1
 
     def flux_x(i):
         a = [sh[0, h, i, ROWS, :] + sh[0, h, i, ABOVE, :] for h in range(2)]
-        up = z_above(a[0], a[1], to_last(z_ax, i))
+        up = z_above(a[0], a[1], to_last(tab[0, 0:N, :], i))
         out = []
         for h in range(2):
             s = 0.25 * (a[h] + up[h])
@@ -655,7 +675,7 @@
             i = x + 1
             t = [sh[1, h, i, wide, :] + sh[1, h, i + 1, wide, :] for h in range(2)]
             ra, rb = [pltpu.roll(v, LANES - 1, 1) for v in t]
-            up = (jnp.where(wide_last, rb, ra), jnp.where(wide_last, to_last(z_y, i), rb))
+            up = (jnp.where(wide_last, rb, ra), jnp.where(wide_last, to_last(tab[1], i), rb))
             for h in range(2):
                 s = 0.25 * (t[h] + up[h])
                 for f, field in enumerate(fields):
@@ -677,22 +697,19 @@
             ]
             for f, field in enumerate(fields):
                 own = [field[h, i, ROWS, :] for h in range(2)]
-                end = to_ends(ends_q[f], i)
+                end = to_ends(tab[2 + f, 0:N, :], i)
                 under = z_below(own[0], own[1], end)
                 g = [s[h] * jnp.where(s[h] > 0, own[h], under[h]) for h in range(2)]
                 over = z_above(g[0], g[1], end)
                 for h in range(2):
                     nr[f, h, x] = nr[f, h, x] + (over[h] - g[h])
         return carry
-    planes(remap_z, 0, 2)
-    for f, out in enumerate((d_out, e_out)):
-        for h in range(2):
-            write(nr.at[f, h], out.at[:, :, halves(h)], 9 + f, h)
-
-    for slot in tuple(sent):
-        drain(slot)
-    for copy in along + across:
-        copy.wait_send()
+    for part in range(4):
+        lo = 8 * part
+        planes(remap_z, 0, 2, lo, lo + 8)
+        for f, out in enumerate((d_out, e_out)):
+            for h in range(2):
+                write(nr.at[f, h, pl.ds(lo, 8)], out.at[pl.ds(lo, 8), :, halves(h)], 9 + 4 * f + part, h)
     for copy in outs:
         copy.wait()
 
@@ -717,16 +734,18 @@
         def body(*refs):
             kernel(sizes, *refs)
 
-        return tuple(pl.pallas_call(
+        in_vmem = pl.BlockSpec(memory_space=pltpu.VMEM)
+        handed = pl.pallas_call(
             body,
             name="lagrangian_step",
-            out_shape=(v3, v3, v3, v1, v1),
+            out_shape=(
+                padded(3), plain(3), plain(3), padded(3), padded(), padded(), pltpu.VMEM((4, 40, LANES), F32)),
             in_specs=[anywhere] * 5,
-            out_specs=[anywhere] * 5,
+            out_specs=[in_vmem] * 7,
             scratch_shapes=[
-                padded(2), plain(), padded(3), padded(3), padded(3), padded(3),
-                plain(3), plain(3), plain(3), plain(dtype=jnp.int32), plain(), plain(), plain(3),
-                padded(3), padded(3), padded(),
+                padded(), plain(), padded(3), padded(3), padded(3),
+                plain(3), plain(3), plain(3), plain(dtype=jnp.int32), plain(), plain(),
+                padded(3), padded(3),
                 pltpu.VMEM((SLOTS, 2, 2, N, 1, LANES), F32),
                 pltpu.VMEM((SLOTS, 2, 2, N, 1, LANES), F32),
                 pltpu.VMEM((SLOTS, N, LANES), F32),
@@ -736,18 +755,26 @@
                 pltpu.VMEM((EDGES, 8, LANES), F32),
                 pltpu.VMEM((EDGES, 8, LANES), F32),
                 pltpu.VMEM((EDGES, PY, LANES), F32),
-                pltpu.VMEM((2, 2, 2, 40, LANES), F32),
                 pltpu.VMEM((16, LANES), F32),
                 pltpu.VMEM((sizes[2], 1, LANES), F32),
                 pltpu.VMEM((sizes[0] * sizes[1], 1, LANES), F32),
-                dma((5, 2)), dma((11, 2)),
+                dma((5, 2)),
                 dma((SLOTS, 6)), dma((SLOTS, 6)), dma((EDGES, 4)), dma((EDGES, 4)),
                 dma((sizes[2],)), dma((sizes[2],)),
                 dma((sizes[0] * sizes[1],)), dma((sizes[0] * sizes[1],)),
             ],
             compiler_params=pltpu.CompilerParams(
-                collective_id=0, has_side_effects=True, vmem_limit_bytes=66 * 1000 * 1000),
-        )(position, velocity, density, energy, pinned))
+                collective_id=0, has_side_effects=True, vmem_limit_bytes=46 * 1000 * 1000),
+        )(position, velocity, density, energy, pinned)
+        return tuple(pl.pallas_call(
+            remap,
+            name="remap",
+            out_shape=(v3, v3, v3, v1, v1),
+            in_specs=[in_vmem] * 7,
+            out_specs=[anywhere] * 5,
+            scratch_shapes=[plain(2), pltpu.VMEM((2, 2, 2, 40, LANES), F32), dma((17, 2))],
+            compiler_params=pltpu.CompilerParams(vmem_limit_bytes=8 * 1000 * 1000),
+        )(*handed))
 
     return jax.shard_map(
         on_device,

time: 83.9 us -> 72.7 us (0.87)
  local copies, waits for them, and re-layouts: 11 us -> 0 us
    unnamed x13 -> x0, local copies, waits for them, and re-layouts: 11 us -> none
    pallas_call x1 -> x2, Pallas kernels: 72 us -> 71.9 us  [the longest x1 63.9 us: on_device(): pl.pallas_call(body, name='lagrangian_step', out_shape=(padded(3), plain(...]
where the time goes in v3:
time: 72.7 us; the launch traced here: 72.6 us
  Pallas kernels  71.9 us (99%)
    pallas_call x1, Pallas kernels, on_device(): pl.pallas_call(body, name='lagrangian_step', out_shape=(padded(3), plain(...  63.9 us
    pallas_call x1, Pallas kernels, on_device(): pl.pallas_call(remap, name='remap', out_shape=(v3, v3, v3, v1, v1), in_sp...  8.08 us

profile of v3, /device:TPU:1, one launch (start us, length us, event | category | flops | bytes accessed | tf_op | source)
XLA Modules:
  0.0 72.6 jit_solution(16658478043769832194)
XLA Ops:
  0.6 63.9 %lagrangian_step.1 = (f32[3,2,34,48,128]{4,3,2,1,0:T(8,128)S(1)}, f32[3,2,32,32,128]{4,3,2,1,0:T(8,128)S(1)}, f32[3,2,32,32,128]{4,3,2,1,0:T(8,128)S(1)}, f32[3,...) custom-call(f32[3,32,32,256]{3,2,1,0:T(8,128)} %refs_0_.1, ...), custom_call_target="tpu_custom_call" | custom-call | tf_op jit(solution)/shard_map/lagrangian_step/pallas_call | solution.py:738
  64.5 8.1 %remap.1 = (f32[3,32,32,256]{3,2,1,0:T(8,128)}, f32[3,32,32,256]{3,2,1,0:T(8,128)}, f32[3,32,32,256]{3,2,1,0:T(8,128)}, f32[32,32,256]{2,1,0:T(8,128)}, f32[32,32,256]{2,1,0:T(8,128)}) custom-call(f32[3,2,34,48,128]{4,3,2,1,0:T(8,128)S(1)} %get-tuple-element.12.vel, f32[3,2,32,32,128]{4,3,2,1,0:T(8,128)S(1)} %get-tuple-element.13.acc, ...), custom_call_target="tpu_custom_call" | custom-call | tf_op jit(solution)/shard_map/remap/pallas_call | solution.py:769

commit v4 on v3

--- a/solution.py
+++ b/solution.py
@@ -11,6 +11,7 @@
 LANES = 128
 PX = N + 2
 PY = 48
+TRIP = 16
 ROWS = pl.ds(8, N)
 BELOW = pl.ds(7, N)
 ABOVE = pl.ds(9, N)
@@ -25,7 +26,7 @@
     return lax.broadcasted_iota(jnp.int32, (N, LANES), 1)
 
 
-def planes(body, init=0, trip=4, start=0, stop=N):
+def planes(body, init=0, trip=TRIP, start=0, stop=N):
     def run(i, carry):
         return body([i * trip + j for j in range(trip)], carry)
     return lax.fori_loop(start // trip, stop // trip, run, init)
@@ -56,9 +57,9 @@
 def kernel(
     sizes,
     pos_in, vel_in, rho_in, en_in, pin_in,
-    vel, acc, relaxed, sh, de, rho_f, tab,
-    pres, en, w, r, q, nw, nr, nq, pin, free, mass, one, two,
-    ys, yr, zs, zr, exy, exz, eyz, exyz, ze, mom, ar1, ar2,
+    vel, acc, relaxed, sh, de, rho_f, tab, partial,
+    pres, en, w, r, q, nw, nr, nq, pin, free, mass, one,
+    ys, yr, zs, zr, exy, exz, eyz, exyz, ze, band, gy, mom, ar1, ar2,
     in_sem, face_s, face_r, edge_s, edge_r, a1s, a1r, a2s, a2r,
 ):
     names = ("bx", "by", "bz")
@@ -85,27 +86,33 @@
     steps = ((-1, 0, 0), (1, 0, 0), (0, -1, 0), (0, 1, 0), (0, 0, -1), (0, 0, 1))
     lane = lax.broadcasted_iota(jnp.int32, (N, LANES), 1)
 
-    def face_copy(slot, field, d):
+    def some(slot, n):
+        return slot if n == 1 else pl.ds(slot, n)
+
+    def face_copy(slot, field, d, n=1):
+        at = some(slot, n)
         if d < 2:
             src, dst = ((1, PX - 1), (N, 0))[d]
-            src, dst = field.at[:, src, ROWS, :], field.at[:, dst, ROWS, :]
+            lead = () if n == 1 else (slice(None),)
+            src, dst = [field.at[lead + (slice(None), plane, ROWS, slice(None))] for plane in (src, dst)]
         elif d < 4:
-            src, dst = ys.at[slot, d - 2], yr.at[slot, 3 - d]
+            src, dst = ys.at[at, d - 2], yr.at[at, 3 - d]
         else:
-            src, dst = zs.at[slot], zr.at[slot, 5 - d]
+            src, dst = zs.at[at], zr.at[at, 5 - d]
         return pltpu.make_async_remote_copy(
             src_ref=src, dst_ref=dst, send_sem=face_s.at[slot, d], recv_sem=face_r.at[slot, d],
             device_id=device(steps[d]), device_id_type=MESH)
 
-    def edge_copies(slot, eslot, sign):
+    def edge_copies(slot, eslot, sign, n=1):
+        at, to = some(slot, n), some(eslot, n)
         side = 1 if sign > 0 else 0
         row = N - 1 if sign > 0 else 0
         tile = pl.ds(N - 8, 8) if sign > 0 else pl.ds(0, 8)
         pieces = (
-            ((sign, sign, 0), ys.at[slot, side, :, row], exy.at[eslot]),
-            ((sign, 0, sign), zs.at[slot], exz.at[eslot]),
-            ((0, sign, sign), zs.at[slot, tile], eyz.at[eslot]),
-            ((sign, sign, sign), zs.at[slot, tile], exyz.at[eslot]),
+            ((sign, sign, 0), ys.at[at, side, :, row], exy.at[to]),
+            ((sign, 0, sign), zs.at[at], exz.at[to]),
+            ((0, sign, sign), zs.at[at, tile], eyz.at[to]),
+            ((sign, sign, sign), zs.at[at, tile], exyz.at[to]),
         )
         return [
             (step, pltpu.make_async_remote_copy(
@@ -116,27 +123,28 @@
 
     sent = {}
 
-    def drain(slot):
-        for step, copy in sent.pop(slot):
-            pl.when(exists(step))(copy.wait_send)
-
-    def send_faces(slot, field, ds=(0, 1, 2, 3, 4, 5)):
+    def drain(*slots):
+        for slot in slots:
+            for step, copy in sent.pop(slot, ()):
+                pl.when(exists(step))(copy.wait_send)
+
+    def send_faces(slot, field, ds=(0, 1, 2, 3, 4, 5), n=1):
         for d in ds:
-            copy = face_copy(slot, field, d)
+            copy = face_copy(slot, field, d, n)
             pl.when(exists(steps[d]))(copy.start)
             sent.setdefault(slot, []).append((steps[d], copy))
 
-    def send_edges(slot, eslot, sign):
-        for step, copy in edge_copies(slot, eslot, sign):
+    def send_edges(slot, eslot, sign, n=1):
+        for step, copy in edge_copies(slot, eslot, sign, n):
             pl.when(exists(step))(copy.start)
             sent.setdefault(slot, []).append((step, copy))
 
-    def wait_faces(slot, field, ds=(0, 1, 2, 3, 4, 5)):
+    def wait_faces(slot, field, ds=(0, 1, 2, 3, 4, 5), n=1):
         for d in ds:
-            pl.when(exists(neg(steps[d])))(face_copy(slot, field, d).wait_recv)
-
-    def wait_edges(slot, eslot, sign):
-        for step, copy in edge_copies(slot, eslot, sign):
+            pl.when(exists(neg(steps[d])))(face_copy(slot, field, d, n).wait_recv)
+
+    def wait_edges(slot, eslot, sign, n=1):
+        for step, copy in edge_copies(slot, eslot, sign, n):
             pl.when(exists(neg(step)))(copy.wait_recv)
 
     zero_plane = jnp.zeros((N, LANES), F32)
@@ -157,7 +165,7 @@
             z = jnp.where((lane >> 1) == x + 1, m, z)
         zs[slot] = z
 
-    def pack_last(slot, field, trip=4):
+    def pack_last(slot, field, trip=TRIP):
         pack_planes(slot, field, list(range(N - trip, N)))
 
     def pack_rows(slot, h, x, v, sides=(0, 1)):
@@ -226,21 +234,31 @@
                 for h in range(2):
                     field[h, plane, ROWS, :] = zero_plane
 
+    at_row = lax.broadcasted_iota(jnp.int32, (2 * LANES, 2 * LANES), 0)
+    at_column = lax.broadcasted_iota(jnp.int32, (2 * LANES, 2 * LANES), 1)
+    band[...] = jnp.where(jnp.abs(at_row - at_column) == 1, 1.0, 0.0).astype(jnp.bfloat16)
+
     def neighbours(field, xs, ends):
-        rolled = []
-        for x in xs:
-            a, b = field[0, x + 1, ROWS, :], field[1, x + 1, ROWS, :]
-            end = to_ends(ends, x + 1)
-            rolled.append((z_below(a, b, end), z_above(a, b, end)))
+        both = [
+            jnp.concatenate([field[h, x + 1, ROWS, :] for x in xs], axis=0) for h in range(2)
+        ]
+        whole = jnp.concatenate(both, axis=1)
+        lead = whole.astype(jnp.bfloat16)
+        rest = (whole - lead.astype(F32)).astype(jnp.bfloat16)
+        along_z = jnp.dot(lead, band[...], preferred_element_type=F32) + jnp.dot(
+            rest, band[...], preferred_element_type=F32)
         out = []
-        for x, (m, p) in zip(xs, rolled):
+        for j, x in enumerate(xs):
             i = x + 1
+            end = to_ends(ends, i)
+            edge = (jnp.where(lane == 0, end, 0.0), jnp.where(lane == LANES - 1, end, 0.0))
             centre = [field[h, i, ROWS, :] for h in range(2)]
             near = []
             for h in range(2):
                 s = (field[h, i - 1, ROWS, :] + field[h, i + 1, ROWS, :]) + (
                     field[h, i, BELOW, :] + field[h, i, ABOVE, :])
-                near.append(s + (m[h] + p[h]))
+                z = along_z[N * j:N * j + N, LANES * h:LANES * h + LANES]
+                near.append(s + (z + edge[h]))
             out.append((x, centre, near))
         return out
 
@@ -268,7 +286,7 @@
     clear_missing(rho_f)
     clear_missing(de)
     for c in range(3):
-        for field in (w, r, q, one, two):
+        for field in (w, r, q, one):
             clear_missing(field.at[c])
         for field in (vel, sh):
             clear_missing(field.at[c], (PX - 1,))
@@ -316,10 +334,10 @@
     pack_last(S_P, pres)
 
     pl.semaphore_wait(barrier, count + (nz - 1) + (nxy - 1))
-    send_edges(S_P, E_P, 1)
-    send_edges(S_RHO, E_RHO, 1)
-    send_faces(S_P, pres, (5, 3, 1))
-    send_faces(S_RHO, rho_f, (5, 3, 1, 4, 2, 0))
+    send_edges(S_P, E_P, 1, 2)
+    send_faces(S_P, None, (5, 3), 2)
+    send_faces(S_P, pres, (1,))
+    send_faces(S_RHO, rho_f, (1, 4, 2, 0))
 
     for name in ("vel", "pos", "pin"):
         for h in range(2):
@@ -336,21 +354,14 @@
             return carry
         planes(body)
         pack_last(S_W + c, w.at[c])
-        send_faces(S_W + c, w.at[c])
 
     for c in range(3):
         advance(c)
 
-    def mask_body(x, _):
-        for h in range(2):
-            free[h, x] = 0.8 - 0.8 * pin[h, x].astype(F32)
-        return 0
-    lax.fori_loop(0, N, mask_body, 0)
-
-    wait_faces(S_P, pres, (5, 3, 1))
-    wait_edges(S_P, E_P, 1)
-    wait_faces(S_RHO, rho_f)
-    wait_edges(S_RHO, E_RHO, 1)
+    wait_faces(S_P, None, (5, 3), 2)
+    wait_edges(S_P, E_P, 1, 2)
+    wait_faces(S_P, pres, (1,))
+    wait_faces(S_RHO, rho_f, (1, 4, 2, 0))
     edge_halo(S_P, E_P, pres, 1)
     edge_halo(S_RHO, E_RHO, rho_f, 1)
     unpack_rows(S_RHO, rho_f, (1,))
@@ -383,6 +394,7 @@
     for c in range(3):
         pack(S_R + c, r.at[c])
         send_faces(S_R + c, r.at[c])
+    send_faces(S_W, w, n=3)
 
     def mass_terms(i):
         ay = [rho_f[h, i, ROWS, :] + rho_f[h, i, BELOW, :] for h in range(2)]
@@ -427,7 +439,8 @@
             mom[4 * c + k:4 * c + k + 1, :] = jnp.sum(m, axis=0, keepdims=True)
 
     def near_w(c):
-        ends = receive(S_W + c, w.at[c])
+        unpack_rows(S_W + c, w.at[c])
+        ends = z_halos(S_W + c)
 
         def body(xs, carry):
             for x, _centre, near in neighbours(w.at[c], xs, ends):
@@ -436,7 +449,6 @@
             return carry
         planes(body)
 
-    near_w(0)
     for c in range(3):
         ends = receive(S_Q + c, q.at[c])
 
@@ -474,11 +486,19 @@
     along = reduce_copies(ar1, a1s, a1r, z_peer, nz)
     for copy in along:
         copy.start()
-    near_w(1)
+    def mask_body(x, _):
+        for h in range(2):
+            free[h, x] = 0.8 - 0.8 * pin[h, x].astype(F32)
+        return 0
+    lax.fori_loop(0, N, mask_body, 0)
+    wait_faces(S_W, w, n=3)
+    drain(S_P, S_RHO, S_W, *range(S_R, S_R + 3), *range(S_Q, S_Q + 3))
+    near_w(0)
     ar2[0] = gathered(ar1, along)
     across = reduce_copies(ar2, a2s, a2r, xy_peer, nxy)
     for copy in across:
         copy.start()
+    near_w(1)
     near_w(2)
     sums = gathered(ar2, across)
     row_lane = lax.broadcasted_iota(jnp.int32, (1, LANES), 1)
@@ -511,14 +531,15 @@
                     one[c, h, i, ROWS, :] = u
                     pack_rows(S_ONE + c, h, x, u)
             return carry
-        drain(S_W + c)
         planes(step_body)
         pack_last(S_ONE + c, one.at[c])
         send_faces(S_ONE + c, one.at[c])
     for c in range(3):
         pack(S_VEL + c, vel.at[c], (0,))
-        send_faces(S_VEL + c, vel.at[c], (0, 2, 4))
-        send_edges(S_VEL + c, E_VEL + c, -1)
+    send_faces(S_VEL, vel, (0, 2, 4), 3)
+    send_edges(S_VEL, E_VEL, -1, 3)
+
+    two = r
 
     def swept(field, c, xs, ends):
         return [
@@ -540,9 +561,9 @@
         pack_last(S_TWO + c, two.at[c])
         send_faces(S_TWO + c, two.at[c])
 
-    for c in range(3):
-        wait_faces(S_VEL + c, vel.at[c], (0, 2, 4))
-        wait_edges(S_VEL + c, E_VEL + c, -1)
+    wait_faces(S_VEL, vel, (0, 2, 4), 3)
+    wait_edges(S_VEL, E_VEL, -1, 3)
+    for c in range(3):
         edge_halo(S_VEL + c, E_VEL + c, vel.at[c], -1)
 
     def rows_up(k):
@@ -604,54 +625,24 @@
         send_faces(S_SH + c, sh.at[c], (4, 2, 0))
         send_edges(S_SH + c, E_SH + c, -1)
 
+    drain(*range(S_ONE, S_ONE + 3), *range(S_TWO, S_TWO + 3), S_VEL, S_DE)
     receive(S_DE, de)
-    for c in range(3):
+    fields = (rho_f, de)
+    wide = pl.ds(8, 40)
+    wide_last = lax.broadcasted_iota(jnp.int32, (40, LANES), 1) == LANES - 1
+
+    def receive_shift(c):
         wait_faces(S_SH + c, sh.at[c], (4, 2, 0))
         wait_edges(S_SH + c, E_SH + c, -1)
         edge_halo(S_SH + c, E_SH + c, sh.at[c], -1)
-    zx, zz3 = rows_up(E_SH), rows_up(E_SH + 2)
-    tab[0, 0:N, :] = zx[0] + zx[1]
-    z_y = ze[E_SH + 1, pl.ds(8, 40), :]
-    tab[1] = z_y + pltpu.roll(z_y, LANES - 2, 1)
-    z_z = zz3[0] + zz3[1]
-    z_z = 0.25 * (z_z + pltpu.roll(z_z, LANES - 2, 1))
-    for f, slot in enumerate((S_RHO, S_DE)):
-        tab[2 + f, 0:N, :] = jnp.where(
-            odd, z_halo(slot, 0), z_z * jnp.where(z_z > 0, z_halo(slot, 1), zs[slot]))
-
-    for slot in tuple(sent):
-        drain(slot)
-    for copy in along + across:
-        copy.wait_send()
-
-
-def remap(
-    vel, acc, relaxed, sh, de, rho_f, tab,
-    v_out, a_out, r_out, d_out, e_out,
-    nr, gy, out_sem,
-):
-    fields = (rho_f, de)
-    wide = pl.ds(8, 40)
-    outs = []
-
-    def halves(k):
-        return pl.ds(k * LANES, LANES)
-
-    def write(src, dst, i, h):
-        copy = pltpu.make_async_copy(src, dst, out_sem.at[i, h])
-        copy.start()
-        outs.append(copy)
-
-    for c in range(3):
-        for h in range(2):
-            write(acc.at[c, h], a_out.at[c, :, :, halves(h)], c, h)
-            write(vel.at[c, h, pl.ds(1, N), ROWS, :], v_out.at[c, :, :, halves(h)], 3 + c, h)
-            write(relaxed.at[c, h], r_out.at[c, :, :, halves(h)], 6 + c, h)
-    wide_last = lax.broadcasted_iota(jnp.int32, (40, LANES), 1) == LANES - 1
+        return rows_up(E_SH + c)
+
+    zx = receive_shift(0)
+    z_ax = zx[0] + zx[1]
 
     def flux_x(i):
         a = [sh[0, h, i, ROWS, :] + sh[0, h, i, ABOVE, :] for h in range(2)]
-        up = z_above(a[0], a[1], to_last(tab[0, 0:N, :], i))
+        up = z_above(a[0], a[1], to_last(z_ax, i))
         out = []
         for h in range(2):
             s = 0.25 * (a[h] + up[h])
@@ -665,17 +656,21 @@
             now = flux_x(x + 2)
             for h in range(2):
                 for f, field in enumerate(fields):
-                    nr[f, h, x] = field[h, x + 1, ROWS, :] + (now[2 * h + f] - before[2 * h + f])
+                    partial[f, h, x] = field[h, x + 1, ROWS, :] + (now[2 * h + f] - before[2 * h + f])
             before = now
         return before
     lax.fori_loop(0, N // 2, remap_x, flux_x(1))
+
+    receive_shift(1)
+    z_y = ze[E_SH + 1, wide, :]
+    z_y = z_y + pltpu.roll(z_y, LANES - 2, 1)
 
     def remap_y(xs, carry):
         for j, x in enumerate(xs):
             i = x + 1
             t = [sh[1, h, i, wide, :] + sh[1, h, i + 1, wide, :] for h in range(2)]
             ra, rb = [pltpu.roll(v, LANES - 1, 1) for v in t]
-            up = (jnp.where(wide_last, rb, ra), jnp.where(wide_last, to_last(tab[1], i), rb))
+            up = (jnp.where(wide_last, rb, ra), jnp.where(wide_last, to_last(z_y, i), rb))
             for h in range(2):
                 s = 0.25 * (t[h] + up[h])
                 for f, field in enumerate(fields):
@@ -683,10 +678,43 @@
         for j, x in enumerate(xs):
             for h in range(2):
                 for f in range(2):
-                    nr[f, h, x] = nr[f, h, x] + (gy[j, f, h, 1:N + 1, :] - gy[j, f, h, 0:N, :])
+                    partial[f, h, x] = partial[f, h, x] + (gy[j, f, h, 1:N + 1, :] - gy[j, f, h, 0:N, :])
         return carry
     planes(remap_y, 0, 2)
 
+    zz3 = receive_shift(2)
+    z_z = zz3[0] + zz3[1]
+    z_z = 0.25 * (z_z + pltpu.roll(z_z, LANES - 2, 1))
+    for f, slot in enumerate((S_RHO, S_DE)):
+        tab[f] = jnp.where(
+            odd, z_halo(slot, 0), z_z * jnp.where(z_z > 0, z_halo(slot, 1), zs[slot]))
+
+    for copy in along + across:
+        copy.wait_send()
+    drain(*sent)
+
+
+def remap(
+    vel, acc, relaxed, sh, de, rho_f, tab, partial,
+    v_out, a_out, r_out, d_out, e_out,
+    nr, out_sem,
+):
+    fields = (rho_f, de)
+    outs = []
+
+    def halves(k):
+        return pl.ds(k * LANES, LANES)
+
+    def write(src, dst, i, h):
+        copy = pltpu.make_async_copy(src, dst, out_sem.at[i, h])
+        copy.start()
+        outs.append(copy)
+
+    for c in range(3):
+        for h in range(2):
+            write(acc.at[c, h], a_out.at[c, :, :, halves(h)], c, h)
+            write(vel.at[c, h, pl.ds(1, N), ROWS, :], v_out.at[c, :, :, halves(h)], 3 + c, h)
+            write(relaxed.at[c, h], r_out.at[c, :, :, halves(h)], 6 + c, h)
     def remap_z(xs, carry):
         for x in xs:
             i = x + 1
@@ -697,12 +725,12 @@
             ]
             for f, field in enumerate(fields):
                 own = [field[h, i, ROWS, :] for h in range(2)]
-                end = to_ends(tab[2 + f, 0:N, :], i)
+                end = to_ends(tab[f], i)
                 under = z_below(own[0], own[1], end)
                 g = [s[h] * jnp.where(s[h] > 0, own[h], under[h]) for h in range(2)]
                 over = z_above(g[0], g[1], end)
                 for h in range(2):
-                    nr[f, h, x] = nr[f, h, x] + (over[h] - g[h])
+                    nr[f, h, x] = partial[f, h, x] + (over[h] - g[h])
         return carry
     for part in range(4):
         lo = 8 * part
@@ -739,13 +767,14 @@
             body,
             name="lagrangian_step",
             out_shape=(
-                padded(3), plain(3), plain(3), padded(3), padded(), padded(), pltpu.VMEM((4, 40, LANES), F32)),
+                padded(3), plain(3), plain(3), padded(3), padded(), padded(), pltpu.VMEM((2, N, LANES), F32),
+                plain(2)),
             in_specs=[anywhere] * 5,
-            out_specs=[in_vmem] * 7,
+            out_specs=[in_vmem] * 8,
             scratch_shapes=[
                 padded(), plain(), padded(3), padded(3), padded(3),
                 plain(3), plain(3), plain(3), plain(dtype=jnp.int32), plain(), plain(),
-                padded(3), padded(3),
+                padded(3),
                 pltpu.VMEM((SLOTS, 2, 2, N, 1, LANES), F32),
                 pltpu.VMEM((SLOTS, 2, 2, N, 1, LANES), F32),
                 pltpu.VMEM((SLOTS, N, LANES), F32),
@@ -755,6 +784,8 @@
                 pltpu.VMEM((EDGES, 8, LANES), F32),
                 pltpu.VMEM((EDGES, 8, LANES), F32),
                 pltpu.VMEM((EDGES, PY, LANES), F32),
+                pltpu.VMEM((2 * LANES, 2 * LANES), jnp.bfloat16),
+                pltpu.VMEM((2, 2, 2, 40, LANES), F32),
                 pltpu.VMEM((16, LANES), F32),
                 pltpu.VMEM((sizes[2], 1, LANES), F32),
                 pltpu.VMEM((sizes[0] * sizes[1], 1, LANES), F32),
@@ -764,16 +795,16 @@
                 dma((sizes[0] * sizes[1],)), dma((sizes[0] * sizes[1],)),
             ],
             compiler_params=pltpu.CompilerParams(
-                collective_id=0, has_side_effects=True, vmem_limit_bytes=46 * 1000 * 1000),
+                collective_id=0, has_side_effects=True, vmem_limit_bytes=42 * 1000 * 1000),
         )(position, velocity, density, energy, pinned)
         return tuple(pl.pallas_call(
             remap,
             name="remap",
             out_shape=(v3, v3, v3, v1, v1),
-            in_specs=[in_vmem] * 7,
+            in_specs=[in_vmem] * 8,
             out_specs=[anywhere] * 5,
-            scratch_shapes=[plain(2), pltpu.VMEM((2, 2, 2, 40, LANES), F32), dma((17, 2))],
-            compiler_params=pltpu.CompilerParams(vmem_limit_bytes=8 * 1000 * 1000),
+            scratch_shapes=[plain(2), dma((17, 2))],
+            compiler_params=pltpu.CompilerParams(vmem_limit_bytes=4 * 1000 * 1000),
         )(*handed))
 
     return jax.shard_map(

time: 72.7 us -> 64.6 us (0.89)
  Pallas kernels: 71.9 us -> 63.9 us
    pallas_call x1, Pallas kernels: 63.9 us -> 59.4 us  [on_device(): pl.pallas_call(body, name='lagrangian_step', out_shape=(padded(3), plain(...]
    pallas_call x1, Pallas kernels: 8.08 us -> 4.5 us  [on_device(): pl.pallas_call(remap, name='remap', out_shape=(v3, v3, v3, v1, v1), in_sp...]
where the time goes in v4:
time: 64.6 us; the launch traced here: 64.5 us
  Pallas kernels  63.9 us (99%)
    pallas_call x1, Pallas kernels, on_device(): pl.pallas_call(body, name='lagrangian_step', out_shape=(padded(3), plain(...  59.4 us
    pallas_call x1, Pallas kernels, on_device(): pl.pallas_call(remap, name='remap', out_shape=(v3, v3, v3, v1, v1), in_sp...  4.5 us

profile of v4, /device:TPU:1, one launch (start us, length us, event | category | flops | bytes accessed | tf_op | source)
XLA Modules:
  0.0 64.5 jit_solution(17022066439986109311)
XLA Ops:
  0.6 59.4 %lagrangian_step.1 = (f32[3,2,34,48,128]{4,3,2,1,0:T(8,128)S(1)}, f32[3,2,32,32,128]{4,3,2,1,0:T(8,128)S(1)}, f32[3,2,32,32,128]{4,3,2,1,0:T(8,128)S(1)}, f32[3,...) custom-call(f32[3,32,32,256]{3,2,1,0:T(8,128)} %refs_0_.1, ...), custom_call_target="tpu_custom_call" | custom-call | tf_op jit(solution)/shard_map/lagrangian_step/pallas_call | solution.py:766
  60.0 4.5 %remap.1 = (f32[3,32,32,256]{3,2,1,0:T(8,128)}, f32[3,32,32,256]{3,2,1,0:T(8,128)}, f32[3,32,32,256]{3,2,1,0:T(8,128)}, f32[32,32,256]{2,1,0:T(8,128)}, f32[32,32,256]{2,1,0:T(8,128)}) custom-call(f32[3,2,34,48,128]{4,3,2,1,0:T(8,128)S(1)} %get-tuple-element.13.vel, f32[3,2,32,32,128]{4,3,2,1,0:T(8,128)S(1)} %get-tuple-element.14.acc, ...), custom_call_target="tpu_custom_call" | custom-call | tf_op jit(solution)/shard_map/remap/pallas_call | solution.py:800

commit v5 on v4

--- a/solution.py
+++ b/solution.py
@@ -183,7 +183,7 @@
                         row = 8 if s == 0 else 7 + N
                         ys[slot, s, h, x] = field[h, x + 1, row:row + 1, :]
             return carry
-        planes(body, 0, 8)
+        planes(body, 0, 16)
 
     def unpack_rows(slot, field, sides=(0, 1)):
         have = [flag((0, -1, 0)), flag((0, 1, 0))]
@@ -354,6 +354,8 @@
             return carry
         planes(body)
         pack_last(S_W + c, w.at[c])
+        if c < 2:
+            send_faces(S_W + c, w.at[c])
 
     for c in range(3):
         advance(c)
@@ -394,7 +396,7 @@
     for c in range(3):
         pack(S_R + c, r.at[c])
         send_faces(S_R + c, r.at[c])
-    send_faces(S_W, w, n=3)
+    send_faces(S_W + 2, w.at[2])
 
     def mass_terms(i):
         ay = [rho_f[h, i, ROWS, :] + rho_f[h, i, BELOW, :] for h in range(2)]
@@ -416,6 +418,17 @@
         unpack_rows(slot, field)
         return z_halos(slot)
 
+    def near_w(c):
+        ends = receive(S_W + c, w.at[c])
+
+        def body(xs, carry):
+            for x, _centre, near in neighbours(w.at[c], xs, ends):
+                for h in range(2):
+                    nw[c, h, x] = near[h]
+            return carry
+        planes(body)
+
+    near_w(0)
     for c in range(3):
         ends = receive(S_R + c, r.at[c])
 
@@ -438,17 +451,6 @@
         for k, m in enumerate(moments):
             mom[4 * c + k:4 * c + k + 1, :] = jnp.sum(m, axis=0, keepdims=True)
 
-    def near_w(c):
-        unpack_rows(S_W + c, w.at[c])
-        ends = z_halos(S_W + c)
-
-        def body(xs, carry):
-            for x, _centre, near in neighbours(w.at[c], xs, ends):
-                for h in range(2):
-                    nw[c, h, x] = near[h]
-            return carry
-        planes(body)
-
     for c in range(3):
         ends = receive(S_Q + c, q.at[c])
 
@@ -462,7 +464,7 @@
         mom[4 * c + 3:4 * c + 4, :] = jnp.sum(m3, axis=0, keepdims=True)
     mom[12:16, :] = jnp.zeros((4, LANES), F32)
 
-    total = jnp.sum(mom[...], axis=1, keepdims=True)
+    total = jnp.sum(mom[0:16, :], axis=1, keepdims=True)
     on_row = lax.broadcasted_iota(jnp.int32, (16, LANES), 0)
     on_lane = lax.broadcasted_iota(jnp.int32, (16, LANES), 1)
     ar1[0] = jnp.sum(jnp.where(on_row == on_lane, total, 0.0), axis=0, keepdims=True)
@@ -491,14 +493,12 @@
             free[h, x] = 0.8 - 0.8 * pin[h, x].astype(F32)
         return 0
     lax.fori_loop(0, N, mask_body, 0)
-    wait_faces(S_W, w, n=3)
-    drain(S_P, S_RHO, S_W, *range(S_R, S_R + 3), *range(S_Q, S_Q + 3))
-    near_w(0)
+    drain(S_P, S_RHO, *range(S_W, S_W + 3), *range(S_R, S_R + 3), *range(S_Q, S_Q + 3))
+    near_w(1)
     ar2[0] = gathered(ar1, along)
     across = reduce_copies(ar2, a2s, a2r, xy_peer, nxy)
     for copy in across:
         copy.start()
-    near_w(1)
     near_w(2)
     sums = gathered(ar2, across)
     row_lane = lax.broadcasted_iota(jnp.int32, (1, LANES), 1)
@@ -592,10 +592,10 @@
         return plus, minus
 
     def div_body(k, before):
-        back = jnp.maximum(2 * k - 2, 0)
-        pack_planes(S_DE, de, [back, back + 1])
-        for j in range(2):
-            x = 2 * k + j
+        back = jnp.maximum(4 * k - 4, 0)
+        pack_planes(S_DE, de, [back + j for j in range(4)])
+        for j in range(4):
+            x = 4 * k + j
             plus, minus = div_terms(x + 2)
             for h in range(2):
                 spread = before[h] + plus[h]
@@ -604,8 +604,8 @@
                 pack_rows(S_DE, h, x, value)
             before = minus
         return tuple(before)
-    lax.fori_loop(0, N // 2, div_body, tuple(div_terms(1)[1]))
-    pack_last(S_DE, de, 2)
+    lax.fori_loop(0, N // 4, div_body, tuple(div_terms(1)[1]))
+    pack_last(S_DE, de, 4)
     send_faces(S_DE, de)
 
     for c in range(3):
@@ -651,15 +651,15 @@
         return tuple(out)
 
     def remap_x(k, before):
-        for j in range(2):
-            x = 2 * k + j
+        for j in range(4):
+            x = 4 * k + j
             now = flux_x(x + 2)
             for h in range(2):
                 for f, field in enumerate(fields):
                     partial[f, h, x] = field[h, x + 1, ROWS, :] + (now[2 * h + f] - before[2 * h + f])
             before = now
         return before
-    lax.fori_loop(0, N // 2, remap_x, flux_x(1))
+    lax.fori_loop(0, N // 4, remap_x, flux_x(1))
 
     receive_shift(1)
     z_y = ze[E_SH + 1, wide, :]
@@ -680,7 +680,7 @@
                 for f in range(2):
                     partial[f, h, x] = partial[f, h, x] + (gy[j, f, h, 1:N + 1, :] - gy[j, f, h, 0:N, :])
         return carry
-    planes(remap_y, 0, 2)
+    planes(remap_y, 0, 4)
 
     zz3 = receive_shift(2)
     z_z = zz3[0] + zz3[1]
@@ -734,7 +734,7 @@
         return carry
     for part in range(4):
         lo = 8 * part
-        planes(remap_z, 0, 2, lo, lo + 8)
+        planes(remap_z, 0, 4, lo, lo + 8)
         for f, out in enumerate((d_out, e_out)):
             for h in range(2):
                 write(nr.at[f, h, pl.ds(lo, 8)], out.at[pl.ds(lo, 8), :, halves(h)], 9 + 4 * f + part, h)
@@ -775,27 +775,27 @@
                 padded(), plain(), padded(3), padded(3), padded(3),
                 plain(3), plain(3), plain(3), plain(dtype=jnp.int32), plain(), plain(),
                 padded(3),
-                pltpu.VMEM((SLOTS, 2, 2, N, 1, LANES), F32),
-                pltpu.VMEM((SLOTS, 2, 2, N, 1, LANES), F32),
+                pltpu.VMEM((SLOTS + 1, 2, 2, N, 1, LANES), F32),
+                pltpu.VMEM((SLOTS + 1, 2, 2, N, 1, LANES), F32),
                 pltpu.VMEM((SLOTS, N, LANES), F32),
                 pltpu.VMEM((SLOTS, 2, N, LANES), F32),
-                pltpu.VMEM((EDGES, 2, 1, LANES), F32),
+                pltpu.VMEM((EDGES + 4, 2, 1, LANES), F32),
                 pltpu.VMEM((EDGES, N, LANES), F32),
                 pltpu.VMEM((EDGES, 8, LANES), F32),
                 pltpu.VMEM((EDGES, 8, LANES), F32),
                 pltpu.VMEM((EDGES, PY, LANES), F32),
                 pltpu.VMEM((2 * LANES, 2 * LANES), jnp.bfloat16),
-                pltpu.VMEM((2, 2, 2, 40, LANES), F32),
-                pltpu.VMEM((16, LANES), F32),
-                pltpu.VMEM((sizes[2], 1, LANES), F32),
-                pltpu.VMEM((sizes[0] * sizes[1], 1, LANES), F32),
+                pltpu.VMEM((4, 2, 2, 40, LANES), F32),
+                pltpu.VMEM((24, LANES), F32),
+                pltpu.VMEM((sizes[2] + 8, 1, LANES), F32),
+                pltpu.VMEM((sizes[0] * sizes[1] + 8, 1, LANES), F32),
                 dma((5, 2)),
                 dma((SLOTS, 6)), dma((SLOTS, 6)), dma((EDGES, 4)), dma((EDGES, 4)),
                 dma((sizes[2],)), dma((sizes[2],)),
                 dma((sizes[0] * sizes[1],)), dma((sizes[0] * sizes[1],)),
             ],
             compiler_params=pltpu.CompilerParams(
-                collective_id=0, has_side_effects=True, vmem_limit_bytes=42 * 1000 * 1000),
+                collective_id=0, has_side_effects=True, vmem_limit_bytes=43 * 1000 * 1000),
         )(position, velocity, density, energy, pinned)
         return tuple(pl.pallas_call(
             remap,

time: 64.6 us -> 62.7 us (0.971)
  Pallas kernels: 63.9 us -> 61.8 us
    pallas_call x1, Pallas kernels: 59.4 us -> 57.3 us  [on_device(): pl.pallas_call(body, name='lagrangian_step', out_shape=(padded(3), plain(...]
where the time goes in v5:
time: 62.7 us; the launch traced here: 62.6 us
  Pallas kernels  61.8 us (99%)
  between operations  0.8 us (1%)
    pallas_call x1, Pallas kernels, on_device(): pl.pallas_call(body, name='lagrangian_step', out_shape=(padded(3), plain(...  57.3 us
    pallas_call x1, Pallas kernels, on_device(): pl.pallas_call(remap, name='remap', out_shape=(v3, v3, v3, v1, v1), in_sp...  4.5 us

profile of v5, /device:TPU:1, one launch (start us, length us, event | category | flops | bytes accessed | tf_op | source)
XLA Modules:
  0.0 62.6 jit_solution(8648455410148196991)
XLA Ops:
  0.6 57.3 %lagrangian_step.1 = (f32[3,2,34,48,128]{4,3,2,1,0:T(8,128)S(1)}, f32[3,2,32,32,128]{4,3,2,1,0:T(8,128)S(1)}, f32[3,2,32,32,128]{4,3,2,1,0:T(8,128)S(1)}, f32[3,...) custom-call(f32[3,32,32,256]{3,2,1,0:T(8,128)} %refs_0_.1, ...), custom_call_target="tpu_custom_call" | custom-call | tf_op jit(solution)/shard_map/lagrangian_step/pallas_call | solution.py:766
  57.9 4.5 %remap.1 = (f32[3,32,32,256]{3,2,1,0:T(8,128)}, f32[3,32,32,256]{3,2,1,0:T(8,128)}, f32[3,32,32,256]{3,2,1,0:T(8,128)}, f32[32,32,256]{2,1,0:T(8,128)}, f32[32,32,256]{2,1,0:T(8,128)}) custom-call(f32[3,2,34,48,128]{4,3,2,1,0:T(8,128)S(1)} %get-tuple-element.13.vel, f32[3,2,32,32,128]{4,3,2,1,0:T(8,128)S(1)} %get-tuple-element.14.acc, ...), custom_call_target="tpu_custom_call" | custom-call | tf_op jit(solution)/shard_map/remap/pallas_call | solution.py:800
